TPU v7x, 32 devices: a whole 2x2x4 slice. The times are simulated.
32 devices in a mesh: dp: 16 (over z, x, core), mp: 2 (over y).
Axes of the slice: x: 2, y: 2, z: 4, core: 2. Of those that a mesh axis runs over, the one named last changes fastest.
Arguments:
- tokens: bfloat16 [80, 1024, 1024], P('dp'), may hold values from -6 to 6
- cotangent: bfloat16 [80, 1024, 1024], P('dp'), may hold values from -6 to 6
- lengths: int32 [80], P('dp'), may hold values from 64 to 1024, as said below
- first_norm_gain: float32 [1024], replicated, may hold values from 0.5 to 1.5
- first_norm_bias: float32 [1024], replicated, may hold values from -2 to 2
- query_key_value_weight: bfloat16 [3, 1024, 1024], P(None, None, 'mp'), may hold values from -0.1875 to 0.1875
- attention_output_weight: bfloat16 [1024, 1024], P('mp'), may hold values from -3 to 3
- attention_output_bias: float32 [1024], replicated, may hold values from -2 to 2
- second_norm_gain: float32 [1024], replicated, may hold values from 0.5 to 1.5
- second_norm_bias: float32 [1024], replicated, may hold values from -2 to 2
- feedforward_up_weight: bfloat16 [1024, 4096], P(None, 'mp'), may hold values from -0.1875 to 0.1875
- feedforward_up_bias: float32 [4096], P('mp'), may hold values from -3 to 3
- feedforward_down_weight: bfloat16 [4096, 1024], P('mp'), may hold values from -0.09375 to 0.09375
- feedforward_down_bias: float32 [1024], replicated, may hold values from -2 to 2
- adapter_down_factor: float32 [2, 1024, 4], replicated, may hold values from -0.1875 to 0.1875
- adapter_up_factor: float32 [2, 4, 1024], replicated, may hold values from -0.3 to 0.3
- down_first_moment: float32 [2, 1024, 4], replicated, may hold values from -0.006 to 0.006
- up_first_moment: float32 [2, 4, 1024], replicated, may hold values from -0.006 to 0.006
- down_second_moment: float32 [2, 1024, 4], replicated, may hold values from 1e-07 to 1e-05
- up_second_moment: float32 [2, 4, 1024], replicated, may hold values from 1e-07 to 1e-05
Outputs:
- block_out: bfloat16 [80, 1024, 1024], P('dp')
- input_grad: bfloat16 [80, 1024, 1024], P('dp')
- new_lora_down: float32 [2, 1024, 4], replicated
- new_lora_up: float32 [2, 4, 1024], replicated
- new_first_down: float32 [2, 1024, 4], replicated
- new_first_up: float32 [2, 4, 1024], replicated
- new_second_down: float32 [2, 1024, 4], replicated
- new_second_up: float32 [2, 4, 1024], replicated
Inputs may be any that keep to these rules, and one draw needn't show every extreme that they name: `lengths`: the first of every 5 sequences (each index of dp's first) has 1024 live tokens.
All inputs are finite; a program needn't handle non-finite values.
Results may differ from a plain program's by a relative error of at most 0.015.
The roundings to bfloat16 on the way count: a program that leaves them out, or rounds other values in their place, can miss the bound.
Values may be sent and summed in bfloat16 or wider, within the bound.
A program may use at most 320 MiB of HBM per device.

v0:
```python
import functools

import jax
import jax.numpy as jnp
from jax import lax
from jax.experimental import pallas as pl
from jax.experimental.pallas import tpu as pltpu
from jax.sharding import PartitionSpec as P

HEAD = 64


def layer_norm(values, norm_gain, norm_shift):
    centre = values - jnp.mean(values, axis=-1, keepdims=True)
    spread = jnp.mean(centre * centre, axis=-1, keepdims=True)
    return centre * lax.rsqrt(spread + 1e-05) * norm_gain + norm_shift


def gelu_tanh(values):
    return (
        0.5
        * values
        * (1.0 + jnp.tanh(0.7978845608028654 * (values + 0.044715 * values * values * values)))
    )


def head_major(matrix, seq_rows, head_count):
    return (
        matrix.reshape(seq_rows, -1, head_count, HEAD)
        .transpose(0, 2, 1, 3)
        .reshape(seq_rows * head_count, -1, HEAD)
    )


def token_major(stacked, seq_rows, head_count):
    return (
        stacked.reshape(seq_rows, head_count, -1, HEAD)
        .transpose(0, 2, 1, 3)
        .reshape(-1, head_count * HEAD)
    )


def masked_scores(query_rows, key_rows, seq_len):
    scores = jnp.einsum(
        "qd,kd->qk", query_rows, key_rows, preferred_element_type=jnp.float32
    ) * HEAD ** (-0.5)
    position = jnp.arange(scores.shape[0])
    allowed = (position[None, :] <= position[:, None]) & (position[None, :] < seq_len)
    return jnp.where(allowed, scores, -1e30)


def attend_forward(pieces):
    query_rows, key_rows, value_token_rows, seq_len = pieces
    scores = masked_scores(query_rows, key_rows, seq_len)
    row_max = jnp.max(scores, axis=-1, keepdims=True)
    weights = jnp.exp(scores - row_max)
    row_sum = jnp.sum(weights, axis=-1, keepdims=True)
    probabilities = (weights / row_sum).astype(jnp.bfloat16)
    head_out = jnp.dot(probabilities, value_token_rows, preferred_element_type=jnp.float32)
    return (head_out, row_max[:, 0] + jnp.log(row_sum[:, 0]))


def attend_backward(pieces):
    query_rows, key_rows, value_token_rows, seq_len, grad_head, log_sums = pieces
    scores = masked_scores(query_rows, key_rows, seq_len)
    probabilities = jnp.exp(scores - log_sums[:, None])
    value_gradient_rows = jnp.einsum(
        "qk,qd->kd",
        probabilities.astype(jnp.bfloat16),
        grad_head,
        preferred_element_type=jnp.float32,
    )
    grad_probs = jnp.einsum(
        "qd,kd->qk", grad_head, value_token_rows, preferred_element_type=jnp.float32
    )
    grad_scores = probabilities * (
        grad_probs - jnp.sum(grad_probs * probabilities, axis=-1, keepdims=True)
    )
    grad_scores = grad_scores.astype(jnp.bfloat16)
    query_gradient_rows = jnp.dot(
        grad_scores, key_rows, preferred_element_type=jnp.float32
    ) * HEAD ** (-0.5)
    grad_keys = jnp.einsum(
        "qk,qd->kd", grad_scores, query_rows, preferred_element_type=jnp.float32
    ) * HEAD ** (-0.5)
    return (query_gradient_rows, grad_keys, value_gradient_rows)


def adam_decay_update(adapter, gradient, first_mom, second_mom):
    first_new = 0.9 * first_mom + 0.1 * gradient
    second_new = 0.999 * second_mom + 0.001 * gradient * gradient
    update = first_new / (1.0 - 0.9**10) / (jnp.sqrt(second_new / (1.0 - 0.999**10)) + 1e-08)
    return (adapter - 0.25 * (update + 0.01 * adapter), first_new, second_new)


def per_device(
    tokens,
    cotangent,
    lengths,
    first_norm_gain,
    first_norm_bias,
    query_key_value_weight,
    attention_output_weight,
    attention_output_bias,
    second_norm_gain,
    second_norm_bias,
    feedforward_up_weight,
    feedforward_up_bias,
    feedforward_down_weight,
    feedforward_down_bias,
    adapter_down_factor,
    adapter_up_factor,
    down_first_moment,
    up_first_moment,
    down_second_moment,
    up_second_moment,
):
    seq_rows, seq_len_all, model_width = tokens.shape
    tok_count = seq_rows * seq_len_all
    groups = lax.axis_size("mp")
    worker_shard = lax.axis_index("mp")
    shard_width = query_key_value_weight.shape[2]
    head_count = shard_width // HEAD
    adapter_rank_size = adapter_down_factor.shape[2]
    tokens_f32 = tokens.reshape(tok_count, model_width).astype(jnp.float32)
    normalized_rows = layer_norm(tokens_f32, first_norm_gain, first_norm_bias).astype(jnp.bfloat16)
    down_reduced = adapter_down_factor.astype(jnp.bfloat16)
    up_reduced = adapter_up_factor.astype(jnp.bfloat16)
    up_columns = lax.dynamic_slice_in_dim(up_reduced, worker_shard * shard_width, shard_width, 2)
    down_pair = jnp.concatenate((down_reduced[0], down_reduced[1]), axis=1)
    adapter_pair = jnp.dot(normalized_rows, down_pair, preferred_element_type=jnp.float32).astype(
        jnp.bfloat16
    )
    adapter_query_delta = adapter_pair[:, :adapter_rank_size]
    adapter_value_delta = adapter_pair[:, adapter_rank_size:]
    query_rows = (
        jnp.dot(normalized_rows, query_key_value_weight[0], preferred_element_type=jnp.float32)
        + 8.0 * jnp.dot(adapter_query_delta, up_columns[0], preferred_element_type=jnp.float32)
    ).astype(jnp.bfloat16)
    key_rows = jnp.dot(
        normalized_rows, query_key_value_weight[1], preferred_element_type=jnp.float32
    ).astype(jnp.bfloat16)
    value_token_rows = (
        jnp.dot(normalized_rows, query_key_value_weight[2], preferred_element_type=jnp.float32)
        + 8.0 * jnp.dot(adapter_value_delta, up_columns[1], preferred_element_type=jnp.float32)
    ).astype(jnp.bfloat16)
    limits = jnp.repeat(lengths, head_count)
    query_heads = head_major(query_rows, seq_rows, head_count)
    key_heads = head_major(key_rows, seq_rows, head_count)
    value_heads = head_major(value_token_rows, seq_rows, head_count)
    head_out, log_sums = lax.map(attend_forward, (query_heads, key_heads, value_heads, limits))
    attended = token_major(head_out, seq_rows, head_count).astype(jnp.bfloat16)
    attn_share = (
        lax.psum_scatter(
            jnp.dot(attended, attention_output_weight, preferred_element_type=jnp.float32),
            "mp",
            scatter_dimension=0,
            tiled=True,
        )
        + attention_output_bias
    )

    def norm_two(values):
        return layer_norm(values, second_norm_gain, second_norm_bias)

    def norm_one(values):
        return layer_norm(values, first_norm_gain, first_norm_bias)

    attn_full = lax.all_gather(attn_share, "mp", axis=0, tiled=True)
    residual = tokens_f32 + attn_full
    normed_two = norm_two(residual).astype(jnp.bfloat16)
    hidden_pre = (
        jnp.dot(normed_two, feedforward_up_weight, preferred_element_type=jnp.float32)
        + feedforward_up_bias
    )
    hidden = gelu_tanh(hidden_pre).astype(jnp.bfloat16)
    mlp_share = (
        lax.psum_scatter(
            jnp.dot(hidden, feedforward_down_weight, preferred_element_type=jnp.float32).astype(
                jnp.bfloat16
            ),
            "mp",
            scatter_dimension=0,
            tiled=True,
        ).astype(jnp.float32)
        + feedforward_down_bias
    )
    mlp_full = lax.all_gather(mlp_share.astype(jnp.bfloat16), "mp", axis=0, tiled=True).astype(
        mlp_share.dtype
    )
    block_out = (residual + mlp_full).astype(jnp.bfloat16)
    live_mask = (jnp.arange(seq_len_all)[None, :] < lengths[:, None]).reshape(tok_count, 1)
    grad_out = jnp.where(
        live_mask, cotangent.reshape(tok_count, model_width), jnp.zeros((), jnp.bfloat16)
    )
    grad_hidden = jnp.einsum(
        "td,fd->tf", grad_out, feedforward_down_weight, preferred_element_type=jnp.float32
    )
    _, gelu_back = jax.vjp(gelu_tanh, hidden_pre)
    grad_pre = gelu_back(grad_hidden)[0].astype(jnp.bfloat16)
    grad_norm2_share = lax.psum_scatter(
        jnp.einsum(
            "tf,df->td", grad_pre, feedforward_up_weight, preferred_element_type=jnp.float32
        ),
        "mp",
        scatter_dimension=0,
        tiled=True,
    )
    grad_norm2 = lax.all_gather(grad_norm2_share, "mp", axis=0, tiled=True)
    _, norm2_back = jax.vjp(norm_two, residual)
    grad_resid = grad_out.astype(jnp.float32) + norm2_back(grad_norm2)[0]
    grad_resid_low = grad_resid.astype(jnp.bfloat16)
    grad_attended = jnp.einsum(
        "td,ed->te", grad_resid_low, attention_output_weight, preferred_element_type=jnp.float32
    ).astype(jnp.bfloat16)
    grad_head = head_major(grad_attended, seq_rows, head_count)
    head_dq, head_dk, head_dv = lax.map(
        attend_backward, (query_heads, key_heads, value_heads, limits, grad_head, log_sums)
    )
    query_gradient_rows = token_major(head_dq, seq_rows, head_count).astype(jnp.bfloat16)
    grad_keys = token_major(head_dk, seq_rows, head_count).astype(jnp.bfloat16)
    value_gradient_rows = token_major(head_dv, seq_rows, head_count).astype(jnp.bfloat16)
    adapter_query_gradient = 8.0 * jnp.einsum(
        "te,re->tr", query_gradient_rows, up_columns[0], preferred_element_type=jnp.float32
    )
    adapter_value_gradient = 8.0 * jnp.einsum(
        "te,re->tr", value_gradient_rows, up_columns[1], preferred_element_type=jnp.float32
    )
    adapter_gradient = jnp.concatenate((adapter_query_gradient, adapter_value_gradient), axis=1)
    down_pair_float32 = down_pair.astype(jnp.float32)
    partial_sum = jnp.einsum(
        "te,de->td",
        query_gradient_rows,
        query_key_value_weight[0],
        preferred_element_type=jnp.float32,
    )
    partial_sum = partial_sum + jnp.einsum(
        "te,de->td", grad_keys, query_key_value_weight[1], preferred_element_type=jnp.float32
    )
    partial_sum = partial_sum + jnp.einsum(
        "te,de->td",
        value_gradient_rows,
        query_key_value_weight[2],
        preferred_element_type=jnp.float32,
    )
    grad_norm1_share = lax.psum_scatter(
        partial_sum
        + jnp.einsum(
            "gy,wy->gw", adapter_gradient, down_pair_float32, precision=lax.Precision.HIGHEST
        ),
        "mp",
        scatter_dimension=0,
        tiled=True,
    )
    grad_down_both = jnp.einsum(
        "fi,fg->ig",
        normalized_rows.astype(jnp.float32),
        adapter_gradient,
        precision=lax.Precision.HIGHEST,
    )
    grad_down = jnp.stack(
        (grad_down_both[:, :adapter_rank_size], grad_down_both[:, adapter_rank_size:])
    )
    grad_up_query = 8.0 * jnp.einsum(
        "zm,zj->mj", adapter_query_delta, query_gradient_rows, preferred_element_type=jnp.float32
    )
    grad_up_value = 8.0 * jnp.einsum(
        "zm,zj->mj", adapter_value_delta, value_gradient_rows, preferred_element_type=jnp.float32
    )
    up_column_gradient = jnp.stack((grad_up_query, grad_up_value))
    grad_up = lax.dynamic_update_slice_in_dim(
        jnp.zeros(adapter_up_factor.shape, jnp.float32),
        up_column_gradient,
        worker_shard * shard_width,
        2,
    )
    live_local = jnp.sum(lengths).astype(jnp.float32)
    down_reduced_sum, up_reduced_sum, live_sum = lax.psum(
        (grad_down, grad_up, live_local), ("dp", "mp")
    )
    active_token_total = live_sum / groups
    grad_norm1 = lax.all_gather(grad_norm1_share, "mp", axis=0, tiled=True)
    _, norm1_back = jax.vjp(norm_one, tokens_f32)
    input_grad = (grad_resid + norm1_back(grad_norm1)[0]).astype(jnp.bfloat16)
    down_factor_next, down_first_moment_next, down_second_moment_next = adam_decay_update(
        adapter_down_factor,
        down_reduced_sum / active_token_total,
        down_first_moment,
        down_second_moment,
    )
    up_factor_next, up_first_moment_next, up_second_moment_next = adam_decay_update(
        adapter_up_factor, up_reduced_sum / active_token_total, up_first_moment, up_second_moment
    )
    return (
        block_out.reshape(seq_rows, seq_len_all, model_width),
        input_grad.reshape(seq_rows, seq_len_all, model_width),
        down_factor_next,
        up_factor_next,
        down_first_moment_next,
        up_first_moment_next,
        down_second_moment_next,
        up_second_moment_next,
    )


TILE = 256
NT = (((1,), (1,)), ((), ()))


def head_lanes(half):
    lane = lax.broadcasted_iota(jnp.int32, (1, 2 * HEAD), 1)
    return (lane >= half * HEAD) & (lane < (half + 1) * HEAD)


def one_head(block, half):
    return jnp.where(head_lanes(half), block, jnp.zeros((), block.dtype))


def edge_allowed(key_start, query_start, seq_len):
    key_at = key_start + lax.broadcasted_iota(jnp.int32, (TILE, TILE), 0)
    query_at = query_start + lax.broadcasted_iota(jnp.int32, (TILE, TILE), 1)
    return (key_at <= query_at) & (key_at < seq_len)


def attention_forward_kernel(lens_ref, q_ref, k_ref, v_ref, out_ref, lse_ref, vt_ref):
    seq_len = lens_ref[pl.program_id(0)]
    live_tiles = (seq_len + TILE - 1) // TILE
    vt_ref[...] = v_ref[0].T
    tiles = q_ref.shape[1] // TILE

    def row_tile(tile, extent):
        rows = pl.ds(tile * TILE, TILE)
        inner = (extent - 1) * TILE
        query = q_ref[0, rows, :] * HEAD ** (-0.5)
        allowed = edge_allowed(inner, tile * TILE, seq_len)
        outs = []
        for half in range(2):
            mine = one_head(query, half)
            edge = lax.dot_general(
                k_ref[0, pl.ds(inner, TILE), :], mine, NT, preferred_element_type=jnp.float32
            )
            edge = jnp.where(allowed, edge, -1e30)
            top = jnp.max(edge, axis=0, keepdims=True)
            if inner:
                past = lax.dot_general(
                    k_ref[0, pl.ds(0, inner), :], mine, NT, preferred_element_type=jnp.float32
                )
                top = jnp.maximum(top, jnp.max(past, axis=0, keepdims=True))
            head_rows = pl.ds(half * HEAD, HEAD)
            edge = jnp.exp(edge - top)
            total = jnp.sum(edge, axis=0, keepdims=True)
            out = jnp.dot(
                vt_ref[head_rows, pl.ds(inner, TILE)],
                edge.astype(jnp.bfloat16),
                preferred_element_type=jnp.float32,
            )
            if inner:
                past = jnp.exp(past - top)
                total = total + jnp.sum(past, axis=0, keepdims=True)
                out = out + jnp.dot(
                    vt_ref[head_rows, pl.ds(0, inner)],
                    past.astype(jnp.bfloat16),
                    preferred_element_type=jnp.float32,
                )
            outs.append(out / total)
            lse_ref[0, 0, pl.ds(half, 1), rows] = top + jnp.log(total)
        out_ref[0, rows, :] = jnp.concatenate(outs, axis=0).T.astype(out_ref.dtype)

    for tile in range(tiles):
        for extent in range(1, tile + 2):
            pl.when(jnp.minimum(live_tiles, tile + 1) == extent)(
                lambda tile=tile, extent=extent: row_tile(tile, extent)
            )


def attention_forward(lens, query, key, value):
    seqs, length, width = query.shape
    pairs = width // (2 * HEAD)
    spec = pl.BlockSpec((1, length, 2 * HEAD), lambda s, h, lens: (s, 0, h))
    return pl.pallas_call(
        attention_forward_kernel,
        grid_spec=pltpu.PrefetchScalarGridSpec(
            num_scalar_prefetch=1,
            grid=(seqs, pairs),
            in_specs=[spec] * 3,
            out_specs=[spec, pl.BlockSpec((1, 1, 2, length), lambda s, h, lens: (s, h, 0, 0))],
            scratch_shapes=[pltpu.VMEM((2 * HEAD, length), jnp.bfloat16)],
        ),
        out_shape=[
            jax.ShapeDtypeStruct(query.shape, jnp.bfloat16),
            jax.ShapeDtypeStruct((seqs, pairs, 2, length), jnp.float32),
        ],
        cost_estimate=pl.CostEstimate(
            flops=seqs * width * length * length * 3,
            bytes_accessed=seqs * width * length * 8,
            transcendentals=seqs * pairs * length * length,
        ),
        name="attention_forward",
    )(lens, query, key, value)


def attention_backward_kernel(
    lens_ref, q_ref, k_ref, v_ref, g_ref, lse_ref, dq_ref, dk_ref, dv_ref, kt_ref, dk_acc, dv_acc
):
    seq_len = lens_ref[pl.program_id(0)]
    kt_ref[...] = k_ref[0].T
    dk_acc[...] = jnp.zeros_like(dk_acc)
    dv_acc[...] = jnp.zeros_like(dv_acc)
    tiles = q_ref.shape[1] // TILE

    def row_tile(tile):
        rows = pl.ds(tile * TILE, TILE)
        inner = tile * TILE
        query = q_ref[0, rows, :] * HEAD ** (-0.5)
        grad = g_ref[rows, :]
        allowed = edge_allowed(inner, inner, seq_len)
        spans = [(inner, TILE)] + ([(0, inner)] if inner else [])
        outs = []
        for half in range(2):
            mine = one_head(query, half)
            mine_grad = one_head(grad, half)
            lse = lse_ref[0, 0, pl.ds(half, 1), rows]
            probs, grad_probs, row_dot = [], [], 0.0
            for at, (start, size) in enumerate(spans):
                keys = pl.ds(start, size)
                scores = lax.dot_general(
                    k_ref[0, keys, :], mine, NT, preferred_element_type=jnp.float32
                )
                if at == 0:
                    scores = jnp.where(allowed, scores, -1e30)
                prob = jnp.exp(scores - lse)
                dv_acc[keys, :] += jnp.dot(
                    prob.astype(jnp.bfloat16), mine_grad, preferred_element_type=jnp.float32
                )
                grad_prob = lax.dot_general(
                    v_ref[0, keys, :], mine_grad, NT, preferred_element_type=jnp.float32
                )
                row_dot = row_dot + jnp.sum(prob * grad_prob, axis=0, keepdims=True)
                probs.append(prob)
                grad_probs.append(grad_prob)
            out = 0.0
            for (start, size), prob, grad_prob in zip(spans, probs, grad_probs):
                keys = pl.ds(start, size)
                grad_scores = (prob * (grad_prob - row_dot)).astype(jnp.bfloat16)
                dk_acc[keys, :] += jnp.dot(grad_scores, mine, preferred_element_type=jnp.float32)
                out = out + jnp.dot(
                    kt_ref[pl.ds(half * HEAD, HEAD), keys],
                    grad_scores,
                    preferred_element_type=jnp.float32,
                )
            outs.append(out)
        dq = jnp.concatenate(outs, axis=0).T * HEAD ** (-0.5)
        dq_ref[0, rows, :] = dq.astype(dq_ref.dtype)

    for tile in range(tiles):
        pl.when(tile * TILE < seq_len)(lambda tile=tile: row_tile(tile))

        @pl.when(tile * TILE >= seq_len)
        def _(tile=tile):
            dq_ref[0, pl.ds(tile * TILE, TILE), :] = jnp.zeros((TILE, 2 * HEAD), dq_ref.dtype)

    dk_ref[0] = dk_acc[...].astype(dk_ref.dtype)
    dv_ref[0] = dv_acc[...].astype(dv_ref.dtype)


def attention_backward(lens, query, key, value, grad, lse, start):
    length, width = query.shape[1:]
    seqs = lens.shape[0]
    pairs = width // (2 * HEAD)

    def block(first):
        return pl.BlockSpec((1, length, 2 * HEAD), lambda s, h, lens: (s + first, 0, h))

    return pl.pallas_call(
        attention_backward_kernel,
        grid_spec=pltpu.PrefetchScalarGridSpec(
            num_scalar_prefetch=1,
            grid=(seqs, pairs),
            in_specs=[block(start)] * 3
            + [
                pl.BlockSpec((length, 2 * HEAD), lambda s, h, lens: (s, h)),
                pl.BlockSpec((1, 1, 2, length), lambda s, h, lens: (s + start, h, 0, 0)),
            ],
            out_specs=[block(0)] * 3,
            scratch_shapes=[
                pltpu.VMEM((2 * HEAD, length), jnp.bfloat16),
                pltpu.VMEM((length, 2 * HEAD), jnp.float32),
                pltpu.VMEM((length, 2 * HEAD), jnp.float32),
            ],
        ),
        out_shape=[jax.ShapeDtypeStruct((seqs, length, width), jnp.bfloat16)] * 3,
        cost_estimate=pl.CostEstimate(
            flops=seqs * width * length * length * 7,
            bytes_accessed=seqs * width * length * 14,
            transcendentals=seqs * pairs * length * length,
        ),
        name="attention_backward",
    )(lens, query, key, value, grad, lse)


MID_ROWS = 256
CHUNK = 1024


def centred(values):
    centre = values - jnp.mean(values, axis=-1, keepdims=True)
    inverse = lax.rsqrt(jnp.mean(centre * centre, axis=-1, keepdims=True) + 1e-05)
    return centre * inverse, inverse


def norm_backward(grad, gain, normal, inverse):
    grad = grad * gain
    mean = jnp.mean(grad, axis=-1, keepdims=True)
    along = jnp.mean(grad * normal, axis=-1, keepdims=True)
    return (grad - mean - normal * along) * inverse


def dot(a, b):
    return jnp.dot(a, b, preferred_element_type=jnp.float32)


def dot_t(a, b):
    return lax.dot_general(a, b, NT, preferred_element_type=jnp.float32)


def copies_of(pairs, sems):
    return [pltpu.make_async_copy(a, b, sems.at[i]) for i, (a, b) in enumerate(pairs)]


def middle_kernel(
    table_ref,
    tokens_ref,
    cotangent_ref,
    attended_own,
    attended_far,
    out_bias_ref,
    gain_ref,
    shift_ref,
    up_bias_ref,
    down_bias_ref,
    out_own,
    out_near,
    out_far,
    up_own,
    up_near,
    up_far,
    down_own,
    down_near,
    down_far,
    block_ref,
    resid_grad_ref,
    own_grad_ref,
    far_grad_ref,
    out_w,
    up_w,
    down_w,
    residual_ref,
    normed_ref,
    normal_ref,
    acc_ref,
    grad_acc_ref,
    sems,
):
    step = pl.program_id(0)

    pairs = []
    start = 0
    for piece in (out_own, out_near, out_far):
        rows = piece.shape[0]
        pairs.append((piece, out_w.at[pl.ds(start, rows), :]))
        start += rows
    chunk = 0
    for up, down in ((up_own, down_own), (up_near, down_near), (up_far, down_far)):
        for at in range(up.shape[1] // CHUNK):
            units = pl.ds(at * CHUNK, CHUNK)
            pairs.append((up.at[:, units], up_w.at[chunk]))
            pairs.append((down.at[units, :], down_w.at[chunk]))
            chunk += 1
    loads = copies_of(pairs, sems)

    @pl.when(step == 0)
    def _():
        for load in loads:
            load.start()
        for load in loads[:3]:
            load.wait()

    live = table_ref[2, step]
    residual = tokens_ref[...].astype(jnp.float32) + (
        dot(jnp.concatenate((attended_own[...], attended_far[...]), axis=1), out_w[...])
        + out_bias_ref[...]
    )
    residual_ref[...] = residual
    normal, inverse = centred(residual)
    normal_ref[...] = normal
    normed_ref[...] = (normal * gain_ref[...] + shift_ref[...]).astype(jnp.bfloat16)
    acc_ref[...] = jnp.zeros_like(acc_ref)

    @pl.when(step == 0)
    def _():
        for load in loads[3:]:
            load.wait()

    scale = 0.7978845608028654
    cube = 0.044715 * scale

    def forward_only(chunk, carry):
        pre = dot(normed_ref[...], up_w[chunk]) + up_bias_ref[chunk]
        tanh = jnp.tanh(pre * (scale + cube * (pre * pre)))
        hidden = (pre * (0.5 + 0.5 * tanh)).astype(jnp.bfloat16)
        acc_ref[...] += dot(hidden, down_w[chunk])
        return carry

    def finish():
        block_ref[...] = (residual_ref[...] + acc_ref[...] + down_bias_ref[...]).astype(
            block_ref.dtype
        )

    @pl.when(live > 0)
    def _():
        row = lax.broadcasted_iota(jnp.int32, (MID_ROWS, 1), 0)
        grad_out = jnp.where(row < live, cotangent_ref[...], jnp.zeros((), jnp.bfloat16))
        grad_acc_ref[...] = jnp.zeros_like(grad_acc_ref)

        def both_ways(chunk, carry):
            pre = dot(normed_ref[...], up_w[chunk]) + up_bias_ref[chunk]
            grad_hidden = dot_t(grad_out, down_w[chunk])
            square = pre * pre
            tanh = jnp.tanh(pre * (scale + cube * square))
            gate = 0.5 + 0.5 * tanh
            hidden = (pre * gate).astype(jnp.bfloat16)
            slope = gate + (pre * (0.5 - 0.5 * (tanh * tanh))) * (scale + 3.0 * cube * square)
            grad_pre = (grad_hidden * slope).astype(jnp.bfloat16)
            acc_ref[...] += dot(hidden, down_w[chunk])
            grad_acc_ref[...] += dot_t(grad_pre, up_w[chunk])
            return carry

        lax.fori_loop(0, up_w.shape[0], both_ways, 0, unroll=UNROLL)
        finish()
        grad_resid = grad_out.astype(jnp.float32) + norm_backward(
            grad_acc_ref[...], gain_ref[...], normal_ref[...], inverse
        )
        low = grad_resid.astype(jnp.bfloat16)
        resid_grad_ref[...] = low
        columns = own_grad_ref.shape[1]
        own_grad_ref[...] = dot_t(low, out_w[:columns]).astype(jnp.bfloat16)
        far_grad_ref[...] = dot_t(low, out_w[columns:]).astype(jnp.bfloat16)

    @pl.when(live <= 0)
    def _():
        lax.fori_loop(0, up_w.shape[0], forward_only, 0, unroll=UNROLL)
        finish()
        resid_grad_ref[...] = jnp.zeros_like(resid_grad_ref)
        own_grad_ref[...] = jnp.zeros_like(own_grad_ref)
        far_grad_ref[...] = jnp.zeros_like(far_grad_ref)


UNROLL = 2


def middle(
    table, tokens, cotangent, own, far, out_bias, gain, shift, up_bias, down_bias, weights
):
    rows, width = table.shape[1] * MID_ROWS, tokens.shape[1]
    columns = far.shape[1]
    units = up_bias.shape[0] * up_bias.shape[2]
    tile = pl.BlockSpec((MID_ROWS, width), lambda i, t: (i, 0))
    picked = pl.BlockSpec((MID_ROWS, width), lambda i, t: (t[0, i], 0))
    part = pl.BlockSpec((MID_ROWS, columns), lambda i, t: (i, 0))
    vector = pl.BlockSpec((1, width), lambda i, t: (0, 0))
    chunks = units // CHUNK
    low = jax.ShapeDtypeStruct((rows, width), jnp.bfloat16)
    thin = jax.ShapeDtypeStruct((rows, columns), jnp.bfloat16)
    wide = pltpu.VMEM((MID_ROWS, width), jnp.float32)
    return pl.pallas_call(
        middle_kernel,
        grid_spec=pltpu.PrefetchScalarGridSpec(
            num_scalar_prefetch=1,
            grid=(rows // MID_ROWS,),
            in_specs=[picked] * 2
            + [pl.BlockSpec((MID_ROWS, columns), lambda i, t, a=a: (t[a, i], 0)) for a in (1, 3)]
            + [vector] * 3
            + [pl.BlockSpec(up_bias.shape, lambda i, t: (0, 0, 0)), vector]
            + [pl.BlockSpec(memory_space=pl.ANY)] * 9,
            out_specs=[tile, tile, part, part],
            scratch_shapes=[
                pltpu.VMEM((width, width), jnp.bfloat16),
                pltpu.VMEM((chunks, width, CHUNK), jnp.bfloat16),
                pltpu.VMEM((chunks, CHUNK, width), jnp.bfloat16),
                wide,
                pltpu.VMEM((MID_ROWS, width), jnp.bfloat16),
                wide,
                wide,
                wide,
                pltpu.SemaphoreType.DMA((3 + 2 * chunks,)),
            ],
        ),
        out_shape=[low, low, thin, thin],
        compiler_params=pltpu.CompilerParams(vmem_limit_bytes=56 << 20),
        cost_estimate=pl.CostEstimate(
            flops=rows * width * (units * 8 + width * 4),
            bytes_accessed=rows * width * 12 + units * width * 4,
            transcendentals=rows * units,
        ),
        name="middle",
    )(
        table,
        tokens,
        cotangent,
        own,
        far,
        out_bias,
        gain,
        shift,
        up_bias,
        down_bias,
        *weights,
    )


PROJECT_ROWS = 256


def qkv_loads(own, near, far, weight_ref, sems):
    pairs = []
    start = 0
    for piece in (own, near, far):
        if piece is not None:
            columns = pl.ds(start, piece.shape[2])
            pairs.append((piece, weight_ref.at[:, :, columns]))
            start += piece.shape[2]
    return copies_of(pairs, sems)


def project_kernel(pieces, table_ref, *refs):
    tokens_ref, gain_ref, shift_ref, down_ref, up_ref = refs[:5]
    weights = list(refs[5 : 5 + pieces]) + [None] * (3 - pieces)
    query_ref, key_ref, value_ref, low_ref, weight_ref, sems = refs[5 + pieces :]
    loads = qkv_loads(*weights, weight_ref, sems)
    first = pl.program_id(0) == 0

    @pl.when(first)
    def _():
        for load in loads:
            load.start()

    normal, _ = centred(tokens_ref[...].astype(jnp.float32))
    normed = (normal * gain_ref[...] + shift_ref[...]).astype(jnp.bfloat16)
    low = dot_t(normed, down_ref[...]).astype(jnp.bfloat16)
    low_ref[...] = low.astype(jnp.float32).T

    @pl.when(first)
    def _():
        for load in loads:
            load.wait()

    query_ref[...] = (dot(normed, weight_ref[0]) + 8.0 * dot(low, up_ref[0])).astype(jnp.bfloat16)
    key_ref[...] = dot(normed, weight_ref[1]).astype(jnp.bfloat16)
    value_ref[...] = (dot(normed, weight_ref[2]) + 8.0 * dot(low, up_ref[1])).astype(jnp.bfloat16)


def project(table, tokens, gain, shift, down, up, *weights):
    rows, width = table.shape[0] * PROJECT_ROWS, tokens.shape[1]
    columns = up.shape[2]
    pairs = down.shape[0]
    out = pl.BlockSpec((PROJECT_ROWS, columns), lambda i, t: (i, 0))
    vector = pl.BlockSpec((1, width), lambda i, t: (0, 0))
    return pl.pallas_call(
        functools.partial(project_kernel, len(weights)),
        grid_spec=pltpu.PrefetchScalarGridSpec(
            num_scalar_prefetch=1,
            grid=(rows // PROJECT_ROWS,),
            in_specs=[
                pl.BlockSpec((PROJECT_ROWS, width), lambda i, t: (t[i], 0)),
                vector,
                vector,
                pl.BlockSpec(down.shape, lambda i, t: (0, 0)),
                pl.BlockSpec(up.shape, lambda i, t: (0, 0, 0)),
            ]
            + [pl.BlockSpec(memory_space=pl.ANY)] * len(weights),
            out_specs=[out] * 3 + [pl.BlockSpec((pairs, PROJECT_ROWS), lambda i, t: (0, i))],
            scratch_shapes=[
                pltpu.VMEM((3, width, columns), jnp.bfloat16),
                pltpu.SemaphoreType.DMA((len(weights),)),
            ],
        ),
        out_shape=[jax.ShapeDtypeStruct((rows, columns), jnp.bfloat16)] * 3
        + [jax.ShapeDtypeStruct((pairs, rows), jnp.float32)],
        cost_estimate=pl.CostEstimate(
            flops=rows * width * columns * 6,
            bytes_accessed=rows * (width + 3 * columns) * 2 + 6 * width * columns,
            transcendentals=rows,
        ),
        name="project",
    )(table, tokens, gain, shift, down, up, *weights)


def first_backward_kernel(
    table_ref,
    tokens_ref,
    resid_grad_ref,
    low_ref,
    query_own,
    key_own,
    value_own,
    query_far,
    key_far,
    value_far,
    gain_ref,
    shift_ref,
    down_ref,
    up_ref,
    own_ref,
    near_ref,
    far_ref,
    input_ref,
    down_grad_ref,
    query_up_ref,
    value_up_ref,
    weight_ref,
    sems,
):
    first = pl.program_id(0) == 0
    loads = qkv_loads(own_ref, near_ref, far_ref, weight_ref, sems)

    @pl.when(first)
    def _():
        for load in loads:
            load.start()
        down_grad_ref[...] = jnp.zeros_like(down_grad_ref)
        query_up_ref[...] = jnp.zeros_like(query_up_ref)
        value_up_ref[...] = jnp.zeros_like(value_up_ref)

    normal, inverse = centred(tokens_ref[...].astype(jnp.float32))
    normed = (normal * gain_ref[...] + shift_ref[...]).astype(jnp.bfloat16)
    query = jnp.concatenate((query_own[...], query_far[...]), axis=1)
    key = jnp.concatenate((key_own[...], key_far[...]), axis=1)
    value = jnp.concatenate((value_own[...], value_far[...]), axis=1)
    adapter = 8.0 * (dot_t(query, up_ref[0]) + dot_t(value, up_ref[1]))
    high = adapter.astype(jnp.bfloat16)
    rest = (adapter - high.astype(jnp.float32)).astype(jnp.bfloat16)
    down_grad_ref[...] += dot(high.astype(jnp.float32).T.astype(jnp.bfloat16), normed) + dot(
        rest.astype(jnp.float32).T.astype(jnp.bfloat16), normed
    )
    low = low_ref[...].astype(jnp.bfloat16)
    query_up_ref[...] += dot(low, query)
    value_up_ref[...] += dot(low, value)

    @pl.when(first)
    def _():
        for load in loads:
            load.wait()

    grad = (
        dot_t(query, weight_ref[0])
        + dot_t(key, weight_ref[1])
        + dot_t(value, weight_ref[2])
        + dot(high, down_ref[...])
        + dot(rest, down_ref[...])
    )
    input_ref[...] = (
        resid_grad_ref[...].astype(jnp.float32)
        + norm_backward(grad, gain_ref[...], normal, inverse)
    ).astype(input_ref.dtype)


def first_backward(
    table, tokens, resid_grad, low, own, far, gain, shift, down, up, weights
):
    tiles = table.shape[1]
    rows, width = tiles * PROJECT_ROWS, tokens.shape[1]
    pairs = down.shape[0]
    columns = own[0].shape[1]
    tile = pl.BlockSpec((PROJECT_ROWS, width), lambda i, t: (t[0, i], 0))
    vector = pl.BlockSpec((1, width), lambda i, t: (0, 0))
    small = pl.BlockSpec((pairs, width), lambda i, t: (0, 0))
    sums = jax.ShapeDtypeStruct((pairs, width), jnp.float32)
    return pl.pallas_call(
        first_backward_kernel,
        grid_spec=pltpu.PrefetchScalarGridSpec(
            num_scalar_prefetch=1,
            grid=(tiles,),
            in_specs=[
                tile,
                pl.BlockSpec((PROJECT_ROWS, width), lambda i, t: (t[1, i], 0)),
                pl.BlockSpec((pairs, PROJECT_ROWS), lambda i, t: (0, t[2, i])),
            ]
            + [pl.BlockSpec((PROJECT_ROWS, columns), lambda i, t: (t[3, i], 0))] * 3
            + [pl.BlockSpec((PROJECT_ROWS, columns), lambda i, t: (i, 0))] * 3
            + [vector, vector, small, pl.BlockSpec(up.shape, lambda i, t: (0, 0, 0))]
            + [pl.BlockSpec(memory_space=pl.ANY)] * 3,
            out_specs=[pl.BlockSpec((PROJECT_ROWS, width), lambda i, t: (i, 0))] + [small] * 3,
            scratch_shapes=[
                pltpu.VMEM((3, width, width), jnp.bfloat16),
                pltpu.SemaphoreType.DMA((3,)),
            ],
        ),
        out_shape=[jax.ShapeDtypeStruct((rows, width), jnp.bfloat16)] + [sums] * 3,
        cost_estimate=pl.CostEstimate(
            flops=rows * width * width * 7,
            bytes_accessed=rows * width * 12 + 6 * width * width,
            transcendentals=rows,
        ),
        name="first_backward",
    )(table, tokens, resid_grad, low, *own, *far, gain, shift, down, up, *weights)


def swap(value):
    return lax.ppermute(value, "mp", [(0, 1), (1, 0)])


def after(value, *earlier):
    return lax.optimization_barrier((value, *earlier))[0]


def core_swap(value):
    return lax.ppermute(value, "dp", [(i, i ^ 1) for i in range(lax.axis_size("dp"))])


def core_half(shard, axis):
    size = shard.shape[axis] // 2
    core = lax.rem(lax.axis_index("dp"), 2)
    return lax.dynamic_slice_in_dim(shard, core * size, size, axis)


def core_order(value, axis):
    size = value.shape[axis] // 2
    core = lax.rem(lax.axis_index("dp"), 2)
    low = lax.slice_in_dim(value, 0, size, axis=axis)
    high = lax.slice_in_dim(value, size, 2 * size, axis=axis)
    return jnp.where(
        core == 0, value, jnp.concatenate((high, low), axis=axis)
    )


def sum_all(value):
    count = lax.axis_size("dp")
    if count & (count - 1):
        return lax.psum(value, ("dp", "mp"))
    bit = 1
    while bit < count:
        value = value + lax.ppermute(value, "dp", [(i, i ^ bit) for i in range(count)])
        bit *= 2
    return value + swap(value)


def per_device_pair(
    tokens,
    cotangent,
    lengths,
    first_norm_gain,
    first_norm_bias,
    query_key_value_weight,
    attention_output_weight,
    attention_output_bias,
    second_norm_gain,
    second_norm_bias,
    feedforward_up_weight,
    feedforward_up_bias,
    feedforward_down_weight,
    feedforward_down_bias,
    adapter_down_factor,
    adapter_up_factor,
    down_first_moment,
    up_first_moment,
    down_second_moment,
    up_second_moment,
):
    return pair_step(tokens, cotangent, lengths, first_norm_gain, first_norm_bias, query_key_value_weight, attention_output_weight, attention_output_bias, second_norm_gain, second_norm_bias, feedforward_up_weight, feedforward_up_bias, feedforward_down_weight, feedforward_down_bias, adapter_down_factor, adapter_up_factor, down_first_moment, up_first_moment, down_second_moment, up_second_moment)


def pair_step(
    tokens,
    cotangent,
    lengths,
    first_norm_gain,
    first_norm_bias,
    query_key_value_weight,
    attention_output_weight,
    attention_output_bias,
    second_norm_gain,
    second_norm_bias,
    feedforward_up_weight,
    feedforward_up_bias,
    feedforward_down_weight,
    feedforward_down_bias,
    adapter_down_factor,
    adapter_up_factor,
    down_first_moment,
    up_first_moment,
    down_second_moment,
    up_second_moment,
):
    f32, bf16 = jnp.float32, jnp.bfloat16
    seqs, length, width = tokens.shape
    rank = adapter_down_factor.shape[2]
    me = lax.axis_index("mp")
    columns = query_key_value_weight.shape[2]
    whole, half = 2, length // 2
    tiles, half_tiles = length // MID_ROWS, half // MID_ROWS

    def row(vector):
        return vector.reshape(1, -1)

    qkv_near = swap(core_half(query_key_value_weight, 2))
    up_bias = jnp.concatenate(
        (feedforward_up_bias, core_order(swap(feedforward_up_bias), 0))
    ).reshape(-1, 1, CHUNK)

    down_low = adapter_down_factor.astype(bf16).transpose(0, 2, 1).reshape(2 * rank, width)
    up_low = adapter_up_factor.astype(bf16)
    blank = jnp.zeros_like(up_low[0])
    up_low = jnp.stack(
        (jnp.concatenate((up_low[0], blank)), jnp.concatenate((blank, up_low[1])))
    )
    up_own = lax.dynamic_slice_in_dim(up_low, me * columns, columns, 2)
    up_other = core_order(
        lax.dynamic_slice_in_dim(up_low, (1 - me) * columns, columns, 2), 2
    )
    up_both = jnp.concatenate((up_own, up_other), axis=2)

    places = jnp.arange(seqs, dtype=jnp.int32)
    longer = (lengths[None, :] > lengths[:, None]) | (
        (lengths[None, :] == lengths[:, None]) & (places[None, :] < places[:, None])
    )
    standing = jnp.sum(longer.astype(jnp.int32), axis=1)
    order = jnp.sum(jnp.where(standing[None, :] == places[:, None], places[None, :], 0), axis=1)
    split = order[0]

    mine = jnp.stack((jnp.where(me == 0, order[1], order[2]), jnp.where(me == 0, order[4], order[3])))
    theirs = jnp.stack(
        (jnp.where(me == 0, order[2], order[1]), jnp.where(me == 0, order[3], order[4]))
    )

    def lens_of(index):
        return jnp.sum(jnp.where(places[None, :] == index[:, None], lengths[None, :], 0), axis=1)

    own_lens = lens_of(mine)
    split_lens = lens_of(split[None])
    three_lens = jnp.concatenate((own_lens, split_lens))
    flat_tokens = tokens.reshape(-1, width)
    flat_cotangent = cotangent.reshape(-1, width)
    step = jnp.arange(whole * tiles, dtype=jnp.int32)
    extra = jnp.arange(half_tiles, dtype=jnp.int32) + me * half_tiles
    whole_table = mine[step // tiles] * tiles + step % tiles
    token_table = jnp.concatenate((whole_table, split * tiles + extra))
    own_table = jnp.concatenate((step, whole * tiles + extra))
    live_table = jnp.concatenate(
        (
            own_lens[step // tiles] - (step % tiles) * MID_ROWS,
            split_lens[0] - extra * MID_ROWS,
        )
    )
    three_table = jnp.concatenate(
        (whole_table, split * tiles + jnp.arange(tiles, dtype=jnp.int32))
    )
    gain_one, shift_one = row(first_norm_gain), row(first_norm_bias)

    def sequences(pieces):
        return [piece.reshape(-1, length, columns) for piece in pieces]

    *own_heads, low = project(
        three_table,
        flat_tokens,
        gain_one,
        shift_one,
        down_low,
        up_own,
        query_key_value_weight,
    )
    own_heads = sequences(own_heads)
    qkv_near = after(qkv_near, own_heads[0])
    qkv_far = core_swap(qkv_near)
    out_near = swap(after(core_half(attention_output_weight, 0), qkv_near))
    up_near = swap(after(core_half(feedforward_up_weight, 1), qkv_near))
    attended_own, lse_own = attention_forward(three_lens, *own_heads)
    sent = lax.dynamic_slice_in_dim(attended_own[whole], (1 - me) * half, half, 0)
    attended_got = swap(core_order(sent, 1))
    qkv_far = after(qkv_far, attended_own)
    down_near = swap(after(core_half(feedforward_down_weight, 0), qkv_far))
    qkv = (query_key_value_weight, qkv_near, qkv_far)
    *far_heads, _ = project(
        whole_table,
        flat_tokens,
        gain_one,
        shift_one,
        down_low,
        up_other,
        qkv_near,
        qkv_far,
    )
    far_heads = sequences(far_heads)
    out_far = core_swap(after(out_near, far_heads[0]))
    up_far = core_swap(after(up_near, far_heads[0]))
    attended_far, lse_far = attention_forward(own_lens, *far_heads)
    down_far = core_swap(after(down_near, attended_far))
    far_all = jnp.concatenate((attended_far.reshape(-1, columns), attended_got), axis=0)
    weights = (
        attention_output_weight,
        out_near,
        out_far,
        feedforward_up_weight,
        up_near,
        up_far,
        feedforward_down_weight,
        down_near,
        down_far,
    )
    middle_table = jnp.stack(
        (token_table, own_table, live_table, jnp.arange(token_table.shape[0], dtype=jnp.int32))
    )

    def run_middle(first, last):
        return middle(
            middle_table[:, first:last],
            flat_tokens,
            flat_cotangent,
            attended_own.reshape(-1, columns),
            far_all,
            row(attention_output_bias),
            row(second_norm_gain),
            row(second_norm_bias),
            up_bias,
            row(feedforward_down_bias),
            weights,
        )

    block_zero, resid_zero, *grads_zero = run_middle(0, tiles)
    block_zero_got = swap(block_zero)
    block_rest, resid_rest, *grads_rest = run_middle(tiles, token_table.shape[0])
    grad_got = swap(core_order(grads_rest[1][length:], 1))
    block_rest_got = swap(block_rest)
    grad_kept = grads_rest[0][length:]
    grad_split = jnp.concatenate(
        (jnp.where(me == 0, grad_kept, grad_got), jnp.where(me == 0, grad_got, grad_kept))
    )

    def flat(pieces):
        return [piece.reshape(-1, columns) for piece in pieces]

    def back_whole(index, grads):
        lens = own_lens[index : index + 1]
        own = attention_backward(lens, *own_heads, grads[0], lse_own, index)
        far = attention_backward(lens, *far_heads, grads[1], lse_far, index)
        return flat(own), flat(far)

    span = jnp.arange(tiles, dtype=jnp.int32)

    def back_first(own, far, table, resid_grad):
        return first_backward(
            table,
            flat_tokens,
            resid_grad,
            low,
            own,
            far,
            gain_one,
            shift_one,
            down_low,
            up_both,
            qkv,
        )

    def whole_rows(index):
        at = index * tiles + span
        return jnp.stack((token_table[at], span, at, span, live_table[at]))

    back_zero = back_whole(0, grads_zero)
    split_own = attention_backward(split_lens, *own_heads, grad_split, lse_own, whole)
    split_sent = jnp.stack(
        [lax.dynamic_slice_in_dim(p[0], (1 - me) * half, half, 0) for p in split_own]
    )
    split_got = swap(core_order(split_sent, 2))
    first_zero = back_first(*back_zero, whole_rows(0), resid_zero)
    send_zero = swap(first_zero[0])
    back_one = back_whole(1, grads_rest)
    first_split = back_first(
        flat(split_own),
        [split_got[i] for i in range(3)],
        jnp.stack(
            (
                split * tiles + extra,
                tiles + extra - me * half_tiles,
                whole * tiles + extra,
                extra,
                split_lens[0] - extra * MID_ROWS,
            )
        ),
        resid_rest,
    )
    send_split = swap(first_split[0])
    first_one = back_first(*back_one, whole_rows(1), resid_rest)
    send_one = swap(first_one[0])

    down_sum, query_sum, value_sum = (
        first_zero[i] + first_split[i] + first_one[i] for i in range(1, 4)
    )
    up_sum = 8.0 * jnp.concatenate((query_sum[:rank], value_sum[rank:]))
    up_mine = up_sum[:, :columns]
    up_theirs = core_order(up_sum[:, columns:], 1)
    up_sum = jnp.concatenate(
        (jnp.where(me == 0, up_mine, up_theirs), jnp.where(me == 0, up_theirs, up_mine)), axis=1
    )
    live_row = jnp.full((8, width), jnp.sum(lengths).astype(f32))
    total = sum_all(jnp.concatenate((down_sum, up_sum, live_row)))
    active = total[-1, 0] / 2
    grad_down = total[: 2 * rank].reshape(2, rank, width).transpose(0, 2, 1) / active
    grad_up = total[2 * rank : 4 * rank].reshape(2, rank, width) / active

    def place(pieces):
        out = jnp.zeros((seqs * length, width), bf16)
        for piece, start in pieces:
            out = lax.dynamic_update_slice_in_dim(out, piece, start, 0)
        return out.reshape(tokens.shape)

    here = split * length + half * me
    there = split * length + half * (1 - me)
    block_out = place(
        (
            (block_zero, mine[0] * length),
            (block_rest[:length], mine[1] * length),
            (block_rest[length:], here),
            (block_zero_got, theirs[0] * length),
            (block_rest_got[:length], theirs[1] * length),
            (block_rest_got[length:], there),
        )
    )
    input_grad = place(
        (
            (first_zero[0], mine[0] * length),
            (first_split[0], here),
            (first_one[0], mine[1] * length),
            (send_zero, theirs[0] * length),
            (send_split, there),
            (send_one, theirs[1] * length),
        )
    )
    new_down = adam_decay_update(
        adapter_down_factor, grad_down, down_first_moment, down_second_moment
    )
    new_up = adam_decay_update(adapter_up_factor, grad_up, up_first_moment, up_second_moment)
    return (
        block_out,
        input_grad,
        new_down[0],
        new_up[0],
        new_down[1],
        new_up[1],
        new_down[2],
        new_up[2],
    )


def solution(mesh):
    in_specs = (
        P("dp", None, None),
        P("dp", None, None),
        P("dp"),
        P(),
        P(),
        P(None, None, "mp"),
        P("mp", None),
        P(),
        P(),
        P(),
        P(None, "mp"),
        P("mp"),
        P("mp", None),
        P(),
        P(),
        P(),
        P(),
        P(),
        P(),
        P(),
    )
    out_specs = (P("dp", None, None), P("dp", None, None), P(), P(), P(), P(), P(), P())
    return jax.shard_map(
        per_device_pair if mesh.shape["mp"] == 2 else per_device,
        mesh=mesh,
        in_specs=in_specs,
        out_specs=out_specs,
        check_vma=False,
    )
```

profile of v0, /device:TPU:1, one launch (start us, length us, event | category | flops | bytes accessed | tf_op | source)
XLA Modules:
  0.0 739.4 jit_solution(3989858086284109998)
XLA Ops:
  11.2 27.0 %project.2 = (bf16[3072,512]{1,0:T(8,128)(2,1)}, bf16[3072,512]{1,0:T(8,128)(2,1)}, bf16[3072,512]{1,0:T(8,128)(2,1)}, f32[8,3072]{1,0:T(8,128)}) custom-call(s32[12]{0:T(128)} %pad_add_fusion.5.table_ref, bf16[5120,1024]{1,0:T(8,128)(2,1)} %bitcast.86, f32[1,1024]{1,0:T(1,128)} %bitcast.102, f32[1,1024]{1,0:T(1,128)} %bitcast.107, ...), custom_call_target="tpu_custom_call" | custom-call | flops 9663676416 | bytes 18874368 | tf_op jit(solution)/shard_map/project/pallas_call | solution.py:768
  44.0 50.5 %attention_forward.2 = (bf16[3,1024,512]{2,1,0:T(8,128)(2,1)}, f32[3,4,2,1024]{3,2,1,0:T(2,128)}) custom-call(s32[3]{0:T(128)} %pad_add_fusion.4.lens_ref, bf16[3,1024,512]{2,1,0:T(8,128)(2,1)} %bitcast.126, bf16[3,1024,512]{2,1,0:T(8,128)(2,1)} %bitcast.130, bf16[3,1024,512]{2,1,0:T(8,128)(2,1)} %bitcast.134), custom_call_target="tpu_custom_call" | custom-call | flops 4831838208 | bytes 12582912 | tf_op jit(solution)/shard_map/attention_forward/pallas_call | solution.py:380
  99.1 4.6 constant_dynamic-slice_fusion.3
  106.7 19.2 %project.3 = (bf16[2048,512]{1,0:T(8,128)(2,1)}, bf16[2048,512]{1,0:T(8,128)(2,1)}, bf16[2048,512]{1,0:T(8,128)(2,1)}, f32[8,2048]{1,0:T(8,128)}) custom-call(s32[8]{0:T(128)} %copy-done.27, bf16[5120,1024]{1,0:T(8,128)(2,1)} %bitcast.87, f32[1,1024]{1,0:T(1,128)} %bitcast.103, f32[1,1024]{1,0:T(1,128)} %bitcast.108, ...), custom_call_target="tpu_custom_call" | custom-call | flops 6442450944 | bytes 13631488 | tf_op jit(solution)/shard_map/project/pallas_call | solution.py:768
  125.9 33.6 %attention_forward.3 = (bf16[2,1024,512]{2,1,0:T(8,128)(2,1)}, f32[2,4,2,1024]{3,2,1,0:T(2,128)}) custom-call(s32[2]{0:T(128)} %copy-done, bf16[2,1024,512]{2,1,0:T(8,128)(2,1)} %bitcast.138, bf16[2,1024,512]{2,1,0:T(8,128)(2,1)} %bitcast.141, bf16[2,1024,512]{2,1,0:T(8,128)(2,1)} %bitcast.144), custom_call_target="tpu_custom_call" | custom-call | flops 3221225472 | bytes 8388608 | tf_op jit(solution)/shard_map/attention_forward/pallas_call | solution.py:380
  159.7 41.2 %collective-permute-done.8.down_near = bf16[1024,1024]{1,0:T(8,128)(2,1)} collective-permute-done((bf16[1024,1024]{1,0:T(8,128)(2,1)}, bf16[1024,1024]{1,0:T(8,128)(2,1)}, u32[]{:S(2)}, u32[]{:S(2)}) %collective-permute-start.8) | collective-permute-done | bytes 2097184 | tf_op jit(solution)/shard_map/ppermute | solution.py:909
  214.4 4.0 collective-permute-done.4.out_near
  222.3 64.0 %middle.3 = (bf16[1536,1024]{1,0:T(8,128)(2,1)}, bf16[1536,1024]{1,0:T(8,128)(2,1)}, bf16[1536,512]{1,0:T(8,128)(2,1)}, bf16[1536,512]{1,0:T(8,128)(2,1)}) custom-call(s32[4,6]{1,0:T(4,128)} %slice.143.table_ref, bf16[5120,1024]{1,0:T(8,128)(2,1)} %bitcast.88, bf16[5120,1024]{1,0:T(8,128)(2,1)} %bitcast.116, bf16[3072,512]{1,0:T(8,128)(2,1)} %bitcast.97, ...), custom_call_target="tpu_custom_call" | custom-call | flops 57982058496 | bytes 35651584 | tf_op jit(solution)/shard_map/middle/pallas_call | solution.py:675
  288.6 5.4 collective-permute-start.12
  294.0 56.4 %middle.2 = (bf16[1024,1024]{1,0:T(8,128)(2,1)}, bf16[1024,1024]{1,0:T(8,128)(2,1)}, bf16[1024,512]{1,0:T(8,128)(2,1)}, bf16[1024,512]{1,0:T(8,128)(2,1)}) custom-call(s32[4,4]{1,0:T(4,128)} %bitcast.100, bf16[5120,1024]{1,0:T(8,128)(2,1)} %bitcast.89, bf16[5120,1024]{1,0:T(8,128)(2,1)} %bitcast.117, bf16[3072,512]{1,0:T(8,128)(2,1)} %bitcast.98, ...), custom_call_target="tpu_custom_call" | custom-call | flops 38654705664 | bytes 29360128 | tf_op jit(solution)/shard_map/middle/pallas_call | solution.py:675
  350.5 29.7 %attention_backward.6 = (bf16[1,1024,512]{2,1,0:T(8,128)(2,1)}, bf16[1,1024,512]{2,1,0:T(8,128)(2,1)}, bf16[1,1024,512]{2,1,0:T(8,128)(2,1)}) custom-call(s32[1]{0:T(128)} %get-tuple-element.150.lens_ref, bf16[2,1024,512]{2,1,0:T(8,128)(2,1)} %bitcast.139, bf16[2,1024,512]{2,1,0:T(8,128)(2,1)} %bitcast.142, bf16[2,1024,512]{2,1,0:T(8,128)(2,1)} %bitcast.145, ...), custom_call_target="tpu_custom_call" | custom-call | flops 3758096384 | bytes 7340032 | tf_op jit(solution)/shard_map/attention_backward/pallas_call | solution.py:474
  380.1 29.2 %attention_backward.5 = (bf16[1,1024,512]{2,1,0:T(8,128)(2,1)}, bf16[1,1024,512]{2,1,0:T(8,128)(2,1)}, bf16[1,1024,512]{2,1,0:T(8,128)(2,1)}) custom-call(s32[1]{0:T(128)} %get-tuple-element.150.lens_ref, bf16[3,1024,512]{2,1,0:T(8,128)(2,1)} %bitcast.127, bf16[3,1024,512]{2,1,0:T(8,128)(2,1)} %bitcast.131, bf16[3,1024,512]{2,1,0:T(8,128)(2,1)} %bitcast.135, ...), custom_call_target="tpu_custom_call" | custom-call | flops 3758096384 | bytes 7340032 | tf_op jit(solution)/shard_map/attention_backward/pallas_call | solution.py:474
  409.4 21.0 %first_backward.3 = (bf16[1024,1024]{1,0:T(8,128)(2,1)}, f32[8,1024]{1,0:T(8,128)}, f32[8,1024]{1,0:T(8,128)}, f32[8,1024]{1,0:T(8,128)}) custom-call(s32[5,4]{1,0:T(8,128)} %stack.81.table_ref, bf16[5120,1024]{1,0:T(8,128)(2,1)} %bitcast.90, bf16[1024,1024]{1,0:T(8,128)(2,1)} %get-tuple-element.80.resid_grad_ref, f32[8,3072]{1,0:T(8,128)} %get-tuple-element.81.low_ref, ...), custom_call_target="tpu_custom_call" | custom-call | flops 7516192768 | bytes 18874368 | tf_op jit(solution)/shard_map/first_backward/pallas_call | solution.py:878
  432.7 29.2 %attention_backward.7 = (bf16[1,1024,512]{2,1,0:T(8,128)(2,1)}, bf16[1,1024,512]{2,1,0:T(8,128)(2,1)}, bf16[1,1024,512]{2,1,0:T(8,128)(2,1)}) custom-call(s32[1]{0:T(128)} %bitcast.13.lens_ref, bf16[3,1024,512]{2,1,0:T(8,128)(2,1)} %bitcast.128, bf16[3,1024,512]{2,1,0:T(8,128)(2,1)} %bitcast.132, bf16[3,1024,512]{2,1,0:T(8,128)(2,1)} %bitcast.136, ...), custom_call_target="tpu_custom_call" | custom-call | flops 3758096384 | bytes 7340032 | tf_op jit(solution)/shard_map/attention_backward/pallas_call | solution.py:474
  467.0 8.3 %attention_backward.8 = (bf16[1,1024,512]{2,1,0:T(8,128)(2,1)}, bf16[1,1024,512]{2,1,0:T(8,128)(2,1)}, bf16[1,1024,512]{2,1,0:T(8,128)(2,1)}) custom-call(s32[1]{0:T(128)} %get-tuple-element.149.lens_ref, bf16[3,1024,512]{2,1,0:T(8,128)(2,1)} %bitcast.129, bf16[3,1024,512]{2,1,0:T(8,128)(2,1)} %bitcast.133, bf16[3,1024,512]{2,1,0:T(8,128)(2,1)} %bitcast.137, ...), custom_call_target="tpu_custom_call" | custom-call | flops 3758096384 | bytes 7340032 | tf_op jit(solution)/shard_map/attention_backward/pallas_call | solution.py:474
  475.4 6.9 collective-permute-start.14
  482.2 8.1 %attention_backward.9 = (bf16[1,1024,512]{2,1,0:T(8,128)(2,1)}, bf16[1,1024,512]{2,1,0:T(8,128)(2,1)}, bf16[1,1024,512]{2,1,0:T(8,128)(2,1)}) custom-call(s32[1]{0:T(128)} %get-tuple-element.149.lens_ref, bf16[2,1024,512]{2,1,0:T(8,128)(2,1)} %bitcast.140, bf16[2,1024,512]{2,1,0:T(8,128)(2,1)} %bitcast.143, bf16[2,1024,512]{2,1,0:T(8,128)(2,1)} %bitcast.146, ...), custom_call_target="tpu_custom_call" | custom-call | flops 3758096384 | bytes 7340032 | tf_op jit(solution)/shard_map/attention_backward/pallas_call | solution.py:474
  490.4 21.2 %first_backward.5 = (bf16[1024,1024]{1,0:T(8,128)(2,1)}, f32[8,1024]{1,0:T(8,128)}, f32[8,1024]{1,0:T(8,128)}, f32[8,1024]{1,0:T(8,128)}) custom-call(s32[5,4]{1,0:T(8,128)} %stack.86.table_ref, bf16[5120,1024]{1,0:T(8,128)(2,1)} %bitcast.91, bf16[1536,1024]{1,0:T(8,128)(2,1)} %get-tuple-element.93.resid_grad_ref, f32[8,3072]{1,0:T(8,128)} %get-tuple-element.81.low_ref, ...), custom_call_target="tpu_custom_call" | custom-call | flops 7516192768 | bytes 18874368 | tf_op jit(solution)/shard_map/first_backward/pallas_call | solution.py:878
  511.6 5.5 collective-permute-start.16
  518.5 5.4 broadcast.221.clone
  526.9 2.6 slice_bitcast_fusion
  529.5 13.0 %first_backward.4 = (bf16[512,1024]{1,0:T(8,128)(2,1)}, f32[8,1024]{1,0:T(8,128)}, f32[8,1024]{1,0:T(8,128)}, f32[8,1024]{1,0:T(8,128)}) custom-call(s32[5,2]{1,0:T(8,128)} %copy.29.table_ref, bf16[5120,1024]{1,0:T(8,128)(2,1)} %bitcast.92, bf16[1536,1024]{1,0:T(8,128)(2,1)} %get-tuple-element.93.resid_grad_ref, f32[8,3072]{1,0:T(8,128)} %get-tuple-element.81.low_ref, ...), custom_call_target="tpu_custom_call" | custom-call | flops 3758096384 | bytes 12582912 | tf_op jit(solution)/shard_map/first_backward/pallas_call | solution.py:878
  546.5 17.9 %collective-permute-start.18 = (f32[24,1024]{1,0:T(8,128)S(1)}, f32[24,1024]{1,0:T(8,128)S(1)}, u32[]{:S(2)}, u32[]{:S(2)}) collective-permute-start(f32[24,1024]{1,0:T(8,128)S(1)} %fusion.15), channel_id=1, source_target_pairs={{0,4},{2,6},{4,0},{6,2},{8,12},{10,14},{12,8},{14,10},{16,20},{18,... | collective-permute-start | bytes 294920 | tf_op jit(solution)/shard_map/ppermute | solution.py:942
  564.4 5.4 broadcast.221.clone.1
  569.8 3.2 constant_dynamic-update-slice_fusion.5
  573.1 2.3 constant_dynamic-update-slice_fusion.4
  578.7 59.9 %collective-permute-done.10 = bf16[1024,1024]{1,0:T(8,128)(2,1)} collective-permute-done((bf16[1024,1024]{1,0:T(8,128)(2,1)}, bf16[1024,1024]{1,0:T(8,128)(2,1)}, u32[]{:S(2)}, u32[]{:S(2)}) %collective-permute-start.10) | collective-permute-done | bytes 2097184 | tf_op jit(solution)/shard_map/ppermute | solution.py:909
  638.6 3.1 constant_dynamic-update-slice_fusion.6
  643.1 3.1 constant_dynamic-update-slice_fusion.2
  646.1 79.4 %collective-permute-done.21 = f32[24,1024]{1,0:T(8,128)S(1)} collective-permute-done((f32[24,1024]{1,0:T(8,128)S(1)}, f32[24,1024]{1,0:T(8,128)S(1)}, u32[]{:S(2)}, u32[]{:S(2)}) %collective-permute-start.21) | collective-permute-done | bytes 98336 | tf_op jit(solution)/shard_map/ppermute | solution.py:909
  730.5 3.1 slice_dynamic-update-slice_fusion
  735.9 3.1 constant_dynamic-update-slice_fusion
  (192 shorter events, 63.4 us)
Async XLA Ops:
  0.7 213.7 %collective-permute-start.3 = (f32[2048]{0:T(1024)}, f32[2048]{0:T(1024)S(1)}, u32[]{:S(2)}, u32[]{:S(2)}) collective-permute-start(f32[2048]{0:T(1024)} %param.31), channel_id=1, source_target_pairs={{0,1},{1,0},{2,3},{3,2},{4,5},{5,4},{6,7},{7,6},{8,9},{9,8},{10,11... | collective-permute-start | bytes 24584 | tf_op jit(solution)/shard_map/ppermute | solution.py:909
  4.3 35.1 %collective-permute-start = (bf16[3,1024,256]{2,1,0:T(8,128)(2,1)S(1)}, bf16[3,1024,256]{2,1,0:T(8,128)(2,1)S(1)}, u32[]{:S(2)}, u32[]{:S(2)}) collective-permute-start(bf16[3,1024,256]{2,1,0:T(8,128)(2,1)S(1)} %constant_dynamic-slice_fusion.6), channel_id=1, source_target_pairs={{0,1},{1,0},{2,3},{3,2},{4,5},{5,4},{6,7},{7,6},{8,9},{9,8},{10,11... | collective-permute-start | bytes 4718600 | tf_op jit(solution)/shard_map/ppermute | solution.py:909
  8.6 97.3 %copy-start.27 = (s32[8]{0:T(128)}, s32[8]{0:T(128)S(1)}, u32[]{:S(2)}) copy-start(s32[8]{0:T(128)S(1)} %multiply_add_fusion.1.table_ref) | copy-start | bytes 100
  39.4 64.4 %collective-permute-start.1 = (bf16[3,1024,256]{2,1,0:T(8,128)(2,1)S(1)}, bf16[3,1024,256]{2,1,0:T(8,128)(2,1)}, u32[]{:S(2)}, u32[]{:S(2)}) collective-permute-start(bf16[3,1024,256]{2,1,0:T(8,128)(2,1)S(1)} %collective-permute-done.refs_5_.near_ref), channel_id=1, source_target_pairs={{0,2},{2,0},{4,6},{6,4},{8,10},{10,8},{12,14},{14,12},{16,18},{18,... | collective-permute-start | bytes 4718600 | tf_op jit(solution)/shard_map/ppermute | solution.py:917
  96.8 123.0 %collective-permute-start.2 = (bf16[512,512]{1,0:T(8,128)(2,1)}, bf16[512,512]{1,0:T(8,128)(2,1)S(1)}, u32[]{:S(2)}, u32[]{:S(2)}) collective-permute-start(bf16[512,512]{1,0:T(8,128)(2,1)} %maximum_select_fusion.1), channel_id=1, source_target_pairs={{0,1},{1,0},{2,3},{3,2},{4,5},{5,4},{6,7},{7,6},{8,9},{9,8},{10,11... | collective-permute-start | bytes 1572872 | tf_op jit(solution)/shard_map/ppermute | solution.py:909
  103.7 55.8 %collective-permute-start.6 = (bf16[1024,1024]{1,0:T(8,128)(2,1)}, bf16[1024,1024]{1,0:T(8,128)(2,1)}, u32[]{:S(2)}, u32[]{:S(2)}) collective-permute-start(bf16[1024,1024]{1,0:T(8,128)(2,1)} %get-tuple-element.74), channel_id=1, source_target_pairs={{0,1},{1,0},{2,3},{3,2},{4,5},{5,4},{6,7},{7,6},{8,9},{9,8},{10,11... | collective-permute-start | bytes 6291464 | tf_op jit(solution)/shard_map/ppermute | solution.py:909
  103.7 97.1 %collective-permute-start.8 = (bf16[1024,1024]{1,0:T(8,128)(2,1)}, bf16[1024,1024]{1,0:T(8,128)(2,1)}, u32[]{:S(2)}, u32[]{:S(2)}) collective-permute-start(bf16[1024,1024]{1,0:T(8,128)(2,1)} %get-tuple-element.76), channel_id=1, source_target_pairs={{0,1},{1,0},{2,3},{3,2},{4,5},{5,4},{6,7},{7,6},{8,9},{9,8},{10,11... | collective-permute-start | bytes 6291464 | tf_op jit(solution)/shard_map/ppermute | solution.py:909
  125.9 76.5 %copy-start.1 = (s32[2]{0:T(128)S(1)}, s32[2]{0:T(128)}, u32[]{:S(2)}) copy-start(s32[2]{0:T(128)} %copy-done) | copy-start | bytes 28
  125.9 77.1 %copy-start.11 = (bf16[2,8,512]{2,1,0:T(8,128)(2,1)S(1)}, bf16[2,8,512]{2,1,0:T(8,128)(2,1)}, u32[]{:S(2)}) copy-start(bf16[2,8,512]{2,1,0:T(8,128)(2,1)} %maximum_select_fusion.3.refs_4_) | copy-start | bytes 49156
  125.9 77.1 %copy-start.12 = (bf16[2,8,512]{2,1,0:T(8,128)(2,1)S(1)}, bf16[2,8,512]{2,1,0:T(8,128)(2,1)}, u32[]{:S(2)}) copy-start(bf16[2,8,512]{2,1,0:T(8,128)(2,1)} %get-tuple-element.142.refs_4_) | copy-start | bytes 49156
  159.6 61.9 %collective-permute-start.7 = (bf16[1024,1024]{1,0:T(8,128)(2,1)}, bf16[1024,1024]{1,0:T(8,128)(2,1)}, u32[]{:S(2)}, u32[]{:S(2)}) collective-permute-start(bf16[1024,1024]{1,0:T(8,128)(2,1)} %collective-permute-done.6.up_near), channel_id=1, source_target_pairs={{0,2},{2,0},{4,6},{6,4},{8,10},{10,8},{12,14},{14,12},{16,18},{18,... | collective-permute-start | bytes 6291464 | tf_op jit(solution)/shard_map/ppermute | solution.py:917
  200.9 20.7 %collective-permute-start.9 = (bf16[1024,1024]{1,0:T(8,128)(2,1)}, bf16[1024,1024]{1,0:T(8,128)(2,1)}, u32[]{:S(2)}, u32[]{:S(2)}) collective-permute-start(bf16[1024,1024]{1,0:T(8,128)(2,1)} %collective-permute-done.8.down_near), channel_id=1, source_target_pairs={{0,2},{2,0},{4,6},{6,4},{8,10},{10,8},{12,14},{14,12},{16,18},{18,... | collective-permute-start | bytes 6291464 | tf_op jit(solution)/shard_map/ppermute | solution.py:917
  204.7 13.6 %collective-permute-start.4 = (bf16[256,1024]{1,0:T(8,128)(2,1)S(1)}, bf16[256,1024]{1,0:T(8,128)(2,1)}, u32[]{:S(2)}, u32[]{:S(2)}) collective-permute-start(bf16[256,1024]{1,0:T(8,128)(2,1)S(1)} %constant_dynamic-slice_fusion.5), channel_id=1, source_target_pairs={{0,1},{1,0},{2,3},{3,2},{4,5},{5,4},{6,7},{7,6},{8,9},{9,8},{10,11... | collective-permute-start | bytes 1572872 | tf_op jit(solution)/shard_map/ppermute | solution.py:909
  218.4 3.2 collective-permute-start.5
  288.6 141.8 %collective-permute-start.12 = (bf16[512,512]{1,0:T(8,128)(2,1)S(1)}, bf16[512,512]{1,0:T(8,128)(2,1)S(1)}, u32[]{:S(2)}, u32[]{:S(2)}) collective-permute-start(bf16[512,512]{1,0:T(8,128)(2,1)S(1)} %maximum_select_fusion.2), channel_id=1, source_target_pairs={{0,1},{1,0},{2,3},{3,2},{4,5},{5,4},{6,7},{7,6},{8,9},{9,8},{10,11... | collective-permute-start | bytes 1572872 | tf_op jit(solution)/shard_map/ppermute | solution.py:909
  467.0 59.9 %collective-permute-start.13 = (bf16[3,512,512]{2,1,0:T(8,128)(2,1)}, bf16[3,512,512]{2,1,0:T(8,128)(2,1)}, u32[]{:S(2)}, u32[]{:S(2)}) collective-permute-start(bf16[3,512,512]{2,1,0:T(8,128)(2,1)} %maximum_select_fusion), channel_id=1, source_target_pairs={{0,1},{1,0},{2,3},{3,2},{4,5},{5,4},{6,7},{7,6},{8,9},{9,8},{10,11... | collective-permute-start | bytes 4718600 | tf_op jit(solution)/shard_map/ppermute | solution.py:909
  475.4 167.7 %collective-permute-start.14 = (bf16[1024,1024]{1,0:T(8,128)(2,1)}, bf16[1024,1024]{1,0:T(8,128)(2,1)}, u32[]{:S(2)}, u32[]{:S(2)}) collective-permute-start(bf16[1024,1024]{1,0:T(8,128)(2,1)} %get-tuple-element.92), channel_id=1, source_target_pairs={{0,1},{1,0},{2,3},{3,2},{4,5},{5,4},{6,7},{7,6},{8,9},{9,8},{10,11... | collective-permute-start | bytes 6291464 | tf_op jit(solution)/shard_map/ppermute | solution.py:909
  511.6 224.3 %collective-permute-start.16 = (bf16[1024,1024]{1,0:T(8,128)(2,1)}, bf16[1024,1024]{1,0:T(8,128)(2,1)}, u32[]{:S(2)}, u32[]{:S(2)}) collective-permute-start(bf16[1024,1024]{1,0:T(8,128)(2,1)} %get-tuple-element.106), channel_id=1, source_target_pairs={{0,1},{1,0},{2,3},{3,2},{4,5},{5,4},{6,7},{7,6},{8,9},{9,8},{10,11... | collective-permute-start | bytes 6291464 | tf_op jit(solution)/shard_map/ppermute | solution.py:909
  517.0 121.5 %collective-permute-start.10 = (bf16[1024,1024]{1,0:T(8,128)(2,1)}, bf16[1024,1024]{1,0:T(8,128)(2,1)}, u32[]{:S(2)}, u32[]{:S(2)}) collective-permute-start(bf16[1024,1024]{1,0:T(8,128)(2,1)} %get-tuple-element.78), channel_id=1, source_target_pairs={{0,1},{1,0},{2,3},{3,2},{4,5},{5,4},{6,7},{7,6},{8,9},{9,8},{10,11... | collective-permute-start | bytes 6291464 | tf_op jit(solution)/shard_map/ppermute | solution.py:909
  517.1 213.4 %collective-permute-start.11 = (bf16[1536,1024]{1,0:T(8,128)(2,1)S(1)}, bf16[1536,1024]{1,0:T(8,128)(2,1)}, u32[]{:S(2)}, u32[]{:S(2)}) collective-permute-start(bf16[1536,1024]{1,0:T(8,128)(2,1)S(1)} %copy-done.2), channel_id=1, source_target_pairs={{0,1},{1,0},{2,3},{3,2},{4,5},{5,4},{6,7},{7,6},{8,9},{9,8},{10,11... | collective-permute-start | bytes 9437192 | tf_op jit(solution)/shard_map/ppermute | solution.py:909
  545.1 1.3 collective-permute-start.17
  546.5 26.6 %collective-permute-start.18 = (f32[24,1024]{1,0:T(8,128)S(1)}, f32[24,1024]{1,0:T(8,128)S(1)}, u32[]{:S(2)}, u32[]{:S(2)}) collective-permute-start(f32[24,1024]{1,0:T(8,128)S(1)} %fusion.15), channel_id=1, source_target_pairs={{0,4},{2,6},{4,0},{6,2},{8,12},{10,14},{12,8},{14,10},{16,20},{18,... | collective-permute-start | bytes 294920 | tf_op jit(solution)/shard_map/ppermute | solution.py:942
  573.1 4.0 collective-permute-start.19
  577.1 151.2 %collective-permute-start.15 = (bf16[512,1024]{1,0:T(8,128)(2,1)}, bf16[512,1024]{1,0:T(8,128)(2,1)}, u32[]{:S(2)}, u32[]{:S(2)}) collective-permute-start(bf16[512,1024]{1,0:T(8,128)(2,1)} %get-tuple-element.99), channel_id=1, source_target_pairs={{0,1},{1,0},{2,3},{3,2},{4,5},{5,4},{6,7},{7,6},{8,9},{9,8},{10,11... | collective-permute-start | bytes 3145736 | tf_op jit(solution)/shard_map/ppermute | solution.py:909
  638.6 4.4 collective-permute-start.20
  641.7 85.2 %copy-start.8 = (f32[2,1024,4]{1,2,0:T(4,128)S(1)}, f32[2,1024,4]{1,2,0:T(4,128)}, u32[]{:S(2)}) copy-start(f32[2,1024,4]{1,2,0:T(4,128)} %param.34) | copy-start | bytes 98308
  641.7 85.2 %copy-start.13 = (f32[2,1024,4]{1,2,0:T(4,128)S(1)}, f32[2,1024,4]{1,2,0:T(4,128)}, u32[]{:S(2)}) copy-start(f32[2,1024,4]{1,2,0:T(4,128)} %param.36) | copy-start | bytes 98308
  641.7 85.2 %copy-start.14 = (f32[2,1024,4]{1,2,0:T(4,128)S(1)}, f32[2,1024,4]{1,2,0:T(4,128)}, u32[]{:S(2)}) copy-start(f32[2,1024,4]{1,2,0:T(4,128)} %param.38) | copy-start | bytes 98308
  641.7 85.9 %copy-start.10 = (f32[2,4,1024]{2,1,0:T(4,128)S(1)}, f32[2,4,1024]{2,1,0:T(4,128)}, u32[]{:S(2)}) copy-start(f32[2,4,1024]{2,1,0:T(4,128)} %param.35) | copy-start | bytes 98308
  641.7 85.9 %copy-start.15 = (f32[2,4,1024]{2,1,0:T(4,128)S(1)}, f32[2,4,1024]{2,1,0:T(4,128)}, u32[]{:S(2)}) copy-start(f32[2,4,1024]{2,1,0:T(4,128)} %param.37) | copy-start | bytes 98308
  641.7 85.9 %copy-start.16 = (f32[2,4,1024]{2,1,0:T(4,128)S(1)}, f32[2,4,1024]{2,1,0:T(4,128)}, u32[]{:S(2)}) copy-start(f32[2,4,1024]{2,1,0:T(4,128)} %param.39) | copy-start | bytes 98308
  643.0 82.6 %collective-permute-start.21 = (f32[24,1024]{1,0:T(8,128)S(1)}, f32[24,1024]{1,0:T(8,128)S(1)}, u32[]{:S(2)}, u32[]{:S(2)}) collective-permute-start(f32[24,1024]{1,0:T(8,128)S(1)} %add.311), channel_id=1, source_target_pairs={{0,1},{1,0},{2,3},{3,2},{4,5},{5,4},{6,7},{7,6},{8,9},{9,8},{10,11... | collective-permute-start | bytes 294920 | tf_op jit(solution)/shard_map/ppermute | solution.py:909
  (19 other events, 410.8 us)
where the time goes:
time: 749 us; the launch traced here: 739 us
  Pallas kernels  411 us (55%)
  waiting for transfers between devices  189 us (25%)
  local copies, waits for them, and re-layouts  64.7 us (9%)
  starting transfers between devices  46.2 us (6%)
  other arithmetic  19.7 us (3%)
  between operations  9.3 us (1%)
    ppermute x14, waiting for transfers between devices, swap(): return lax.ppermute(value, 'mp', [(0, 1), (1, 0)])  186 us
    pallas_call x2, Pallas kernels, middle(): pl.pallas_call(middle_kernel, grid_spec=pltpu.PrefetchScalarGridSpec(num_...  120 us
    pallas_call x5, Pallas kernels, attention_backward(): pl.pallas_call(attention_backward_kernel, grid_spec=pltpu.PrefetchScalarG...  104 us
    pallas_call x2, Pallas kernels, attention_forward(): pl.pallas_call(attention_forward_kernel, grid_spec=pltpu.PrefetchScalarGr...  84.1 us
    pallas_call x3, Pallas kernels, first_backward(): pl.pallas_call(first_backward_kernel, grid_spec=pltpu.PrefetchScalarGridS...  55.2 us
    pallas_call x2, Pallas kernels, project(): pl.pallas_call(functools.partial(project_kernel, len(weights)), grid_spec...  46.3 us
    dynamic_update_slice x12, local copies, waits for them, and re-layouts, place(): out = lax.dynamic_update_slice_in_dim(out, piece, start, 0)  27.9 us
    ppermute x14, starting transfers between devices, swap(): return lax.ppermute(value, 'mp', [(0, 1), (1, 0)])  24.8 us
  transfers between devices with their start and end apart: 22, of which 8 were waited for; matrix products, arithmetic and copies ran while one was open for 10% of the time, Pallas kernels for 43%

commit v1 on v0

--- a/solution.py
+++ b/solution.py
@@ -331,39 +331,40 @@
     def row_tile(tile, extent):
         rows = pl.ds(tile * TILE, TILE)
         inner = (extent - 1) * TILE
-        query = q_ref[0, rows, :] * HEAD ** (-0.5)
+        query = both_heads(q_ref[0, rows, :] * HEAD ** (-0.5))
         allowed = edge_allowed(inner, tile * TILE, seq_len)
-        outs = []
-        for half in range(2):
-            mine = one_head(query, half)
-            edge = lax.dot_general(
-                k_ref[0, pl.ds(inner, TILE), :], mine, NT, preferred_element_type=jnp.float32
-            )
-            edge = jnp.where(allowed, edge, -1e30)
-            top = jnp.max(edge, axis=0, keepdims=True)
-            if inner:
-                past = lax.dot_general(
-                    k_ref[0, pl.ds(0, inner), :], mine, NT, preferred_element_type=jnp.float32
-                )
-                top = jnp.maximum(top, jnp.max(past, axis=0, keepdims=True))
-            head_rows = pl.ds(half * HEAD, HEAD)
-            edge = jnp.exp(edge - top)
-            total = jnp.sum(edge, axis=0, keepdims=True)
-            out = jnp.dot(
-                vt_ref[head_rows, pl.ds(inner, TILE)],
-                edge.astype(jnp.bfloat16),
+        allowed = jnp.concatenate((allowed, allowed), axis=1)
+        scores = []
+        for span in range(extent):
+            part = lax.dot_general(
+                k_ref[0, pl.ds(span * TILE, TILE), :],
+                query,
+                NT,
                 preferred_element_type=jnp.float32,
             )
-            if inner:
-                past = jnp.exp(past - top)
-                total = total + jnp.sum(past, axis=0, keepdims=True)
-                out = out + jnp.dot(
-                    vt_ref[head_rows, pl.ds(0, inner)],
-                    past.astype(jnp.bfloat16),
+            if span == extent - 1:
+                part = jnp.where(allowed, part, -1e30)
+            scores.append(part)
+        top = functools.reduce(
+            jnp.maximum, [jnp.max(part, axis=0, keepdims=True) for part in scores]
+        )
+        total, outs = 0.0, [0.0, 0.0]
+        for span, part in enumerate(scores):
+            part = jnp.exp(part - top)
+            total = total + jnp.sum(part, axis=0, keepdims=True)
+            part = part.astype(jnp.bfloat16)
+            for half in range(2):
+                outs[half] = outs[half] + jnp.dot(
+                    vt_ref[pl.ds(half * HEAD, HEAD), pl.ds(span * TILE, TILE)],
+                    part[:, half * TILE : (half + 1) * TILE],
                     preferred_element_type=jnp.float32,
                 )
-            outs.append(out / total)
-            lse_ref[0, 0, pl.ds(half, 1), rows] = top + jnp.log(total)
+        lse = top + jnp.log(total)
+        scale = 1.0 / total
+        for half in range(2):
+            columns = slice(half * TILE, (half + 1) * TILE)
+            outs[half] = outs[half] * scale[:, columns]
+            lse_ref[0, 0, pl.ds(half, 1), rows] = lse[:, columns]
         out_ref[0, rows, :] = jnp.concatenate(outs, axis=0).T.astype(out_ref.dtype)
 
     for tile in range(tiles):
@@ -399,8 +400,24 @@
     )(lens, query, key, value)
 
 
+def both_heads(block):
+    return jnp.concatenate((one_head(block, 0), one_head(block, 1)), axis=0)
+
+
 def attention_backward_kernel(
-    lens_ref, q_ref, k_ref, v_ref, g_ref, lse_ref, dq_ref, dk_ref, dv_ref, kt_ref, dk_acc, dv_acc
+    lens_ref,
+    q_ref,
+    k_ref,
+    v_ref,
+    g_ref,
+    out_ref,
+    lse_ref,
+    dq_ref,
+    dk_ref,
+    dv_ref,
+    kt_ref,
+    dk_acc,
+    dv_acc,
 ):
     seq_len = lens_ref[pl.program_id(0)]
     kt_ref[...] = k_ref[0].T
@@ -410,45 +427,45 @@
 
     def row_tile(tile):
         rows = pl.ds(tile * TILE, TILE)
-        inner = tile * TILE
-        query = q_ref[0, rows, :] * HEAD ** (-0.5)
+        query = both_heads(q_ref[0, rows, :] * HEAD ** (-0.5))
         grad = g_ref[rows, :]
-        allowed = edge_allowed(inner, inner, seq_len)
-        spans = [(inner, TILE)] + ([(0, inner)] if inner else [])
-        outs = []
-        for half in range(2):
-            mine = one_head(query, half)
-            mine_grad = one_head(grad, half)
-            lse = lse_ref[0, 0, pl.ds(half, 1), rows]
-            probs, grad_probs, row_dot = [], [], 0.0
-            for at, (start, size) in enumerate(spans):
-                keys = pl.ds(start, size)
-                scores = lax.dot_general(
-                    k_ref[0, keys, :], mine, NT, preferred_element_type=jnp.float32
-                )
-                if at == 0:
-                    scores = jnp.where(allowed, scores, -1e30)
-                prob = jnp.exp(scores - lse)
-                dv_acc[keys, :] += jnp.dot(
-                    prob.astype(jnp.bfloat16), mine_grad, preferred_element_type=jnp.float32
-                )
-                grad_prob = lax.dot_general(
-                    v_ref[0, keys, :], mine_grad, NT, preferred_element_type=jnp.float32
-                )
-                row_dot = row_dot + jnp.sum(prob * grad_prob, axis=0, keepdims=True)
-                probs.append(prob)
-                grad_probs.append(grad_prob)
-            out = 0.0
-            for (start, size), prob, grad_prob in zip(spans, probs, grad_probs):
-                keys = pl.ds(start, size)
-                grad_scores = (prob * (grad_prob - row_dot)).astype(jnp.bfloat16)
-                dk_acc[keys, :] += jnp.dot(grad_scores, mine, preferred_element_type=jnp.float32)
-                out = out + jnp.dot(
+        product = (grad.astype(jnp.float32) * out_ref[0, rows, :].astype(jnp.float32)).T
+        grad = both_heads(grad)
+
+        def head_pair(pick):
+            return jnp.concatenate([pick(half) for half in range(2)], axis=1)
+
+        lse = head_pair(lambda half: lse_ref[0, 0, pl.ds(half, 1), rows])
+        row_dot = head_pair(
+            lambda half: jnp.sum(
+                product[half * HEAD : (half + 1) * HEAD], axis=0, keepdims=True
+            )
+        )
+        allowed = edge_allowed(0, 0, seq_len - tile * TILE)
+        allowed = jnp.concatenate((allowed, allowed), axis=1)
+        outs = [0.0, 0.0]
+        for span in range(tile + 1):
+            keys = pl.ds(span * TILE, TILE)
+            scores = lax.dot_general(
+                k_ref[0, keys, :], query, NT, preferred_element_type=jnp.float32
+            )
+            if span == tile:
+                scores = jnp.where(allowed, scores, -1e30)
+            prob = jnp.exp(scores - lse)
+            grad_prob = lax.dot_general(
+                v_ref[0, keys, :], grad, NT, preferred_element_type=jnp.float32
+            )
+            grad_scores = (prob * (grad_prob - row_dot)).astype(jnp.bfloat16)
+            dv_acc[keys, :] += jnp.dot(
+                prob.astype(jnp.bfloat16), grad, preferred_element_type=jnp.float32
+            )
+            dk_acc[keys, :] += jnp.dot(grad_scores, query, preferred_element_type=jnp.float32)
+            for half in range(2):
+                outs[half] = outs[half] + jnp.dot(
                     kt_ref[pl.ds(half * HEAD, HEAD), keys],
-                    grad_scores,
+                    grad_scores[:, half * TILE : (half + 1) * TILE],
                     preferred_element_type=jnp.float32,
                 )
-            outs.append(out)
         dq = jnp.concatenate(outs, axis=0).T * HEAD ** (-0.5)
         dq_ref[0, rows, :] = dq.astype(dq_ref.dtype)
 
@@ -463,7 +480,7 @@
     dv_ref[0] = dv_acc[...].astype(dv_ref.dtype)
 
 
-def attention_backward(lens, query, key, value, grad, lse, start):
+def attention_backward(lens, query, key, value, grad, out, lse, start):
     length, width = query.shape[1:]
     seqs = lens.shape[0]
     pairs = width // (2 * HEAD)
@@ -479,6 +496,7 @@
             in_specs=[block(start)] * 3
             + [
                 pl.BlockSpec((length, 2 * HEAD), lambda s, h, lens: (s, h)),
+                block(start),
                 pl.BlockSpec((1, 1, 2, length), lambda s, h, lens: (s + start, h, 0, 0)),
             ],
             out_specs=[block(0)] * 3,
@@ -495,7 +513,7 @@
             transcendentals=seqs * pairs * length * length,
         ),
         name="attention_backward",
-    )(lens, query, key, value, grad, lse)
+    )(lens, query, key, value, grad, out, lse)
 
 
 MID_ROWS = 256
@@ -1140,8 +1158,8 @@
 
     def back_whole(index, grads):
         lens = own_lens[index : index + 1]
-        own = attention_backward(lens, *own_heads, grads[0], lse_own, index)
-        far = attention_backward(lens, *far_heads, grads[1], lse_far, index)
+        own = attention_backward(lens, *own_heads, grads[0], attended_own, lse_own, index)
+        far = attention_backward(lens, *far_heads, grads[1], attended_far, lse_far, index)
         return flat(own), flat(far)
 
     span = jnp.arange(tiles, dtype=jnp.int32)
@@ -1166,7 +1184,7 @@
         return jnp.stack((token_table[at], span, at, span, live_table[at]))
 
     back_zero = back_whole(0, grads_zero)
-    split_own = attention_backward(split_lens, *own_heads, grad_split, lse_own, whole)
+    split_own = attention_backward(split_lens, *own_heads, grad_split, attended_own, lse_own, whole)
     split_sent = jnp.stack(
         [lax.dynamic_slice_in_dim(p[0], (1 - me) * half, half, 0) for p in split_own]
     )

time: 749 us -> 711 us (0.949)
  Pallas kernels: 411 us -> 364 us
  waiting for transfers between devices: 189 us -> 207 us
  starting transfers between devices: 46.2 us -> 37.4 us
    pallas_call x5, Pallas kernels: 104 us -> 75.4 us  [attention_backward(): pl.pallas_call(attention_backward_kernel, grid_spec=pltpu.PrefetchScalarG...]
    ppermute x14, waiting for transfers between devices: 186 us -> 204 us  [swap(): return lax.ppermute(value, 'mp', [(0, 1), (1, 0)])]
    pallas_call x2, Pallas kernels: 84.1 us -> 66.8 us  [attention_forward(): pl.pallas_call(attention_forward_kernel, grid_spec=pltpu.PrefetchScalarGr...]
  transfers between devices with their start and end apart: 22 -> 22, of which waited for: 8 -> 9; matrix products, arithmetic and copies ran while one was open for 10% -> 10% of each run, Pallas kernels for 43% -> 40%
where the time goes in v1:
time: 711 us; the launch traced here: 702 us
  Pallas kernels  364 us (51%)
  waiting for transfers between devices  207 us (29%)
  local copies, waits for them, and re-layouts  64.8 us (9%)
  starting transfers between devices  37.4 us (5%)
  other arithmetic  19.3 us (3%)
  between operations  9.32 us (1%)
    ppermute x14, waiting for transfers between devices, swap(): return lax.ppermute(value, 'mp', [(0, 1), (1, 0)])  204 us
    pallas_call x2, Pallas kernels, middle(): pl.pallas_call(middle_kernel, grid_spec=pltpu.PrefetchScalarGridSpec(num_...  121 us
    pallas_call x5, Pallas kernels, attention_backward(): pl.pallas_call(attention_backward_kernel, grid_spec=pltpu.PrefetchScalarG...  75.4 us
    pallas_call x2, Pallas kernels, attention_forward(): pl.pallas_call(attention_forward_kernel, grid_spec=pltpu.PrefetchScalarGr...  66.8 us
    pallas_call x3, Pallas kernels, first_backward(): pl.pallas_call(first_backward_kernel, grid_spec=pltpu.PrefetchScalarGridS...  55.1 us
    pallas_call x2, Pallas kernels, project(): pl.pallas_call(functools.partial(project_kernel, len(weights)), grid_spec...  46.3 us
    dynamic_update_slice x12, local copies, waits for them, and re-layouts, place(): out = lax.dynamic_update_slice_in_dim(out, piece, start, 0)  27.9 us
    ppermute x14, starting transfers between devices, swap(): return lax.ppermute(value, 'mp', [(0, 1), (1, 0)])  18.7 us
  transfers between devices with their start and end apart: 22, of which 9 were waited for; matrix products, arithmetic and copies ran while one was open for 10% of the time, Pallas kernels for 40%

profile of v1, /device:TPU:1, one launch (start us, length us, event | category | flops | bytes accessed | tf_op | source)
XLA Modules:
  0.0 702.3 jit_solution(7414768052989858013)
XLA Ops:
  11.1 27.0 %project.2 = (bf16[3072,512]{1,0:T(8,128)(2,1)}, bf16[3072,512]{1,0:T(8,128)(2,1)}, bf16[3072,512]{1,0:T(8,128)(2,1)}, f32[8,3072]{1,0:T(8,128)}) custom-call(s32[12]{0:T(128)} %pad_add_fusion.5.table_ref, bf16[5120,1024]{1,0:T(8,128)(2,1)} %bitcast.86, f32[1,1024]{1,0:T(1,128)} %bitcast.114, f32[1,1024]{1,0:T(1,128)} %bitcast.119, ...), custom_call_target="tpu_custom_call" | custom-call | flops 9663676416 | bytes 18874368 | tf_op jit(solution)/shard_map/project/pallas_call | solution.py:786
  43.9 40.3 %attention_forward.2 = (bf16[3,1024,512]{2,1,0:T(8,128)(2,1)}, f32[3,4,2,1024]{3,2,1,0:T(2,128)}) custom-call(s32[3]{0:T(128)} %pad_add_fusion.4.lens_ref, bf16[3,1024,512]{2,1,0:T(8,128)(2,1)} %bitcast.95, bf16[3,1024,512]{2,1,0:T(8,128)(2,1)} %bitcast.99, bf16[3,1024,512]{2,1,0:T(8,128)(2,1)} %bitcast.103), custom_call_target="tpu_custom_call" | custom-call | flops 4831838208 | bytes 12582912 | tf_op jit(solution)/shard_map/attention_forward/pallas_call | solution.py:381
  88.3 4.8 constant_dynamic-slice_fusion.3
  95.9 19.2 %project.3 = (bf16[2048,512]{1,0:T(8,128)(2,1)}, bf16[2048,512]{1,0:T(8,128)(2,1)}, bf16[2048,512]{1,0:T(8,128)(2,1)}, f32[8,2048]{1,0:T(8,128)}) custom-call(s32[8]{0:T(128)} %copy-done.27, bf16[5120,1024]{1,0:T(8,128)(2,1)} %bitcast.87, f32[1,1024]{1,0:T(1,128)} %bitcast.115, f32[1,1024]{1,0:T(1,128)} %bitcast.120, ...), custom_call_target="tpu_custom_call" | custom-call | flops 6442450944 | bytes 13631488 | tf_op jit(solution)/shard_map/project/pallas_call | solution.py:786
  115.2 26.5 %attention_forward.3 = (bf16[2,1024,512]{2,1,0:T(8,128)(2,1)}, f32[2,4,2,1024]{3,2,1,0:T(2,128)}) custom-call(s32[2]{0:T(128)} %copy-done, bf16[2,1024,512]{2,1,0:T(8,128)(2,1)} %bitcast.141, bf16[2,1024,512]{2,1,0:T(8,128)(2,1)} %bitcast.144, bf16[2,1024,512]{2,1,0:T(8,128)(2,1)} %bitcast.147), custom_call_target="tpu_custom_call" | custom-call | flops 3221225472 | bytes 8388608 | tf_op jit(solution)/shard_map/attention_forward/pallas_call | solution.py:381
  141.7 3.5 collective-permute-done.6.up_near
  146.5 43.6 %collective-permute-done.8.down_near = bf16[1024,1024]{1,0:T(8,128)(2,1)} collective-permute-done((bf16[1024,1024]{1,0:T(8,128)(2,1)}, bf16[1024,1024]{1,0:T(8,128)(2,1)}, u32[]{:S(2)}, u32[]{:S(2)}) %collective-permute-start.8) | collective-permute-done | bytes 2097184 | tf_op jit(solution)/shard_map/ppermute | solution.py:927
  203.8 4.0 collective-permute-done.4.out_near
  211.7 64.1 %middle.3 = (bf16[1536,1024]{1,0:T(8,128)(2,1)}, bf16[1536,1024]{1,0:T(8,128)(2,1)}, bf16[1536,512]{1,0:T(8,128)(2,1)}, bf16[1536,512]{1,0:T(8,128)(2,1)}) custom-call(s32[4,6]{1,0:T(4,128)} %slice.143.table_ref, bf16[5120,1024]{1,0:T(8,128)(2,1)} %bitcast.88, bf16[5120,1024]{1,0:T(8,128)(2,1)} %bitcast.128, bf16[3072,512]{1,0:T(8,128)(2,1)} %bitcast.93, ...), custom_call_target="tpu_custom_call" | custom-call | flops 57982058496 | bytes 35651584 | tf_op jit(solution)/shard_map/middle/pallas_call | solution.py:693
  278.1 5.4 collective-permute-start.12
  283.6 56.7 %middle.2 = (bf16[1024,1024]{1,0:T(8,128)(2,1)}, bf16[1024,1024]{1,0:T(8,128)(2,1)}, bf16[1024,512]{1,0:T(8,128)(2,1)}, bf16[1024,512]{1,0:T(8,128)(2,1)}) custom-call(s32[4,4]{1,0:T(4,128)} %bitcast.112, bf16[5120,1024]{1,0:T(8,128)(2,1)} %bitcast.89, bf16[5120,1024]{1,0:T(8,128)(2,1)} %bitcast.129, bf16[3072,512]{1,0:T(8,128)(2,1)} %bitcast.94, ...), custom_call_target="tpu_custom_call" | custom-call | flops 38654705664 | bytes 29360128 | tf_op jit(solution)/shard_map/middle/pallas_call | solution.py:693
  340.3 20.5 %attention_backward.6 = (bf16[1,1024,512]{2,1,0:T(8,128)(2,1)}, bf16[1,1024,512]{2,1,0:T(8,128)(2,1)}, bf16[1,1024,512]{2,1,0:T(8,128)(2,1)}) custom-call(s32[1]{0:T(128)} %get-tuple-element.150.lens_ref, bf16[2,1024,512]{2,1,0:T(8,128)(2,1)} %bitcast.142, bf16[2,1024,512]{2,1,0:T(8,128)(2,1)} %bitcast.145, bf16[2,1024,512]{2,1,0:T(8,128)(2,1)} %bitcast.148, ...), custom_call_target="tpu_custom_call" | custom-call | flops 3758096384 | bytes 7340032 | tf_op jit(solution)/shard_map/attention_backward/pallas_call | solution.py:491
  360.8 20.4 %attention_backward.5 = (bf16[1,1024,512]{2,1,0:T(8,128)(2,1)}, bf16[1,1024,512]{2,1,0:T(8,128)(2,1)}, bf16[1,1024,512]{2,1,0:T(8,128)(2,1)}) custom-call(s32[1]{0:T(128)} %get-tuple-element.150.lens_ref, bf16[3,1024,512]{2,1,0:T(8,128)(2,1)} %bitcast.96, bf16[3,1024,512]{2,1,0:T(8,128)(2,1)} %bitcast.100, bf16[3,1024,512]{2,1,0:T(8,128)(2,1)} %bitcast.104, ...), custom_call_target="tpu_custom_call" | custom-call | flops 3758096384 | bytes 7340032 | tf_op jit(solution)/shard_map/attention_backward/pallas_call | solution.py:491
  381.1 20.8 %first_backward.3 = (bf16[1024,1024]{1,0:T(8,128)(2,1)}, f32[8,1024]{1,0:T(8,128)}, f32[8,1024]{1,0:T(8,128)}, f32[8,1024]{1,0:T(8,128)}) custom-call(s32[5,4]{1,0:T(8,128)} %stack.81.table_ref, bf16[5120,1024]{1,0:T(8,128)(2,1)} %bitcast.90, bf16[1024,1024]{1,0:T(8,128)(2,1)} %get-tuple-element.80.resid_grad_ref, f32[8,3072]{1,0:T(8,128)} %get-tuple-element.81.low_ref, ...), custom_call_target="tpu_custom_call" | custom-call | flops 7516192768 | bytes 18874368 | tf_op jit(solution)/shard_map/first_backward/pallas_call | solution.py:896
  404.1 20.6 %attention_backward.7 = (bf16[1,1024,512]{2,1,0:T(8,128)(2,1)}, bf16[1,1024,512]{2,1,0:T(8,128)(2,1)}, bf16[1,1024,512]{2,1,0:T(8,128)(2,1)}) custom-call(s32[1]{0:T(128)} %bitcast.13.lens_ref, bf16[3,1024,512]{2,1,0:T(8,128)(2,1)} %bitcast.97, bf16[3,1024,512]{2,1,0:T(8,128)(2,1)} %bitcast.101, bf16[3,1024,512]{2,1,0:T(8,128)(2,1)} %bitcast.105, ...), custom_call_target="tpu_custom_call" | custom-call | flops 3758096384 | bytes 7340032 | tf_op jit(solution)/shard_map/attention_backward/pallas_call | solution.py:491
  429.9 6.9 attention_backward.8
  436.8 4.1 collective-permute-start.14
  440.9 7.1 %attention_backward.9 = (bf16[1,1024,512]{2,1,0:T(8,128)(2,1)}, bf16[1,1024,512]{2,1,0:T(8,128)(2,1)}, bf16[1,1024,512]{2,1,0:T(8,128)(2,1)}) custom-call(s32[1]{0:T(128)} %get-tuple-element.149.lens_ref, bf16[2,1024,512]{2,1,0:T(8,128)(2,1)} %bitcast.143, bf16[2,1024,512]{2,1,0:T(8,128)(2,1)} %bitcast.146, bf16[2,1024,512]{2,1,0:T(8,128)(2,1)} %bitcast.149, ...), custom_call_target="tpu_custom_call" | custom-call | flops 3758096384 | bytes 7340032 | tf_op jit(solution)/shard_map/attention_backward/pallas_call | solution.py:491
  447.9 21.0 %first_backward.5 = (bf16[1024,1024]{1,0:T(8,128)(2,1)}, f32[8,1024]{1,0:T(8,128)}, f32[8,1024]{1,0:T(8,128)}, f32[8,1024]{1,0:T(8,128)}) custom-call(s32[5,4]{1,0:T(8,128)} %stack.86.table_ref, bf16[5120,1024]{1,0:T(8,128)(2,1)} %bitcast.91, bf16[1536,1024]{1,0:T(8,128)(2,1)} %get-tuple-element.93.resid_grad_ref, f32[8,3072]{1,0:T(8,128)} %get-tuple-element.81.low_ref, ...), custom_call_target="tpu_custom_call" | custom-call | flops 7516192768 | bytes 18874368 | tf_op jit(solution)/shard_map/first_backward/pallas_call | solution.py:896
  468.9 2.7 collective-permute-start.16
  473.1 5.4 broadcast.221.clone
  481.5 2.5 slice_bitcast_fusion
  484.1 13.3 %first_backward.4 = (bf16[512,1024]{1,0:T(8,128)(2,1)}, f32[8,1024]{1,0:T(8,128)}, f32[8,1024]{1,0:T(8,128)}, f32[8,1024]{1,0:T(8,128)}) custom-call(s32[5,2]{1,0:T(8,128)} %copy.29.table_ref, bf16[5120,1024]{1,0:T(8,128)(2,1)} %bitcast.92, bf16[1536,1024]{1,0:T(8,128)(2,1)} %get-tuple-element.93.resid_grad_ref, f32[8,3072]{1,0:T(8,128)} %get-tuple-element.81.low_ref, ...), custom_call_target="tpu_custom_call" | custom-call | flops 3758096384 | bytes 12582912 | tf_op jit(solution)/shard_map/first_backward/pallas_call | solution.py:896
  501.2 13.7 %collective-permute-start.18 = (f32[24,1024]{1,0:T(8,128)S(1)}, f32[24,1024]{1,0:T(8,128)S(1)}, u32[]{:S(2)}, u32[]{:S(2)}) collective-permute-start(f32[24,1024]{1,0:T(8,128)S(1)} %fusion.15), channel_id=1, source_target_pairs={{0,4},{2,6},{4,0},{6,2},{8,12},{10,14},{12,8},{14,10},{16,20},{18,... | collective-permute-start | bytes 294920 | tf_op jit(solution)/shard_map/ppermute | solution.py:960
  515.0 5.4 broadcast.221.clone.1
  520.4 3.2 constant_dynamic-update-slice_fusion.5
  529.2 72.2 %collective-permute-done.10 = bf16[1024,1024]{1,0:T(8,128)(2,1)} collective-permute-done((bf16[1024,1024]{1,0:T(8,128)(2,1)}, bf16[1024,1024]{1,0:T(8,128)(2,1)}, u32[]{:S(2)}, u32[]{:S(2)}) %collective-permute-start.10) | collective-permute-done | bytes 2097184 | tf_op jit(solution)/shard_map/ppermute | solution.py:927
  601.5 3.1 constant_dynamic-update-slice_fusion.6
  605.9 3.1 constant_dynamic-update-slice_fusion.2
  609.0 79.4 %collective-permute-done.21 = f32[24,1024]{1,0:T(8,128)S(1)} collective-permute-done((f32[24,1024]{1,0:T(8,128)S(1)}, f32[24,1024]{1,0:T(8,128)S(1)}, u32[]{:S(2)}, u32[]{:S(2)}) %collective-permute-start.21) | collective-permute-done | bytes 98336 | tf_op jit(solution)/shard_map/ppermute | solution.py:927
  693.4 3.1 slice_dynamic-update-slice_fusion
  698.7 3.1 constant_dynamic-update-slice_fusion
  (192 shorter events, 66.2 us)
Async XLA Ops:
  0.7 203.1 %collective-permute-start.3 = (f32[2048]{0:T(1024)}, f32[2048]{0:T(1024)S(1)}, u32[]{:S(2)}, u32[]{:S(2)}) collective-permute-start(f32[2048]{0:T(1024)} %param.31), channel_id=1, source_target_pairs={{0,1},{1,0},{2,3},{3,2},{4,5},{5,4},{6,7},{7,6},{8,9},{9,8},{10,11... | collective-permute-start | bytes 24584 | tf_op jit(solution)/shard_map/ppermute | solution.py:927
  4.3 35.1 %collective-permute-start = (bf16[3,1024,256]{2,1,0:T(8,128)(2,1)S(1)}, bf16[3,1024,256]{2,1,0:T(8,128)(2,1)S(1)}, u32[]{:S(2)}, u32[]{:S(2)}) collective-permute-start(bf16[3,1024,256]{2,1,0:T(8,128)(2,1)S(1)} %constant_dynamic-slice_fusion.6), channel_id=1, source_target_pairs={{0,1},{1,0},{2,3},{3,2},{4,5},{5,4},{6,7},{7,6},{8,9},{9,8},{10,11... | collective-permute-start | bytes 4718600 | tf_op jit(solution)/shard_map/ppermute | solution.py:927
  8.6 86.6 %copy-start.27 = (s32[8]{0:T(128)}, s32[8]{0:T(128)S(1)}, u32[]{:S(2)}) copy-start(s32[8]{0:T(128)S(1)} %multiply_add_fusion.1.table_ref) | copy-start | bytes 100
  39.4 54.0 %collective-permute-start.1 = (bf16[3,1024,256]{2,1,0:T(8,128)(2,1)S(1)}, bf16[3,1024,256]{2,1,0:T(8,128)(2,1)}, u32[]{:S(2)}, u32[]{:S(2)}) collective-permute-start(bf16[3,1024,256]{2,1,0:T(8,128)(2,1)S(1)} %collective-permute-done.refs_5_.near_ref), channel_id=1, source_target_pairs={{0,2},{2,0},{4,6},{6,4},{8,10},{10,8},{12,14},{14,12},{16,18},{18,... | collective-permute-start | bytes 4718600 | tf_op jit(solution)/shard_map/ppermute | solution.py:935
  86.5 122.8 %collective-permute-start.2 = (bf16[512,512]{1,0:T(8,128)(2,1)}, bf16[512,512]{1,0:T(8,128)(2,1)S(1)}, u32[]{:S(2)}, u32[]{:S(2)}) collective-permute-start(bf16[512,512]{1,0:T(8,128)(2,1)} %maximum_select_fusion.1), channel_id=1, source_target_pairs={{0,1},{1,0},{2,3},{3,2},{4,5},{5,4},{6,7},{7,6},{8,9},{9,8},{10,11... | collective-permute-start | bytes 1572872 | tf_op jit(solution)/shard_map/ppermute | solution.py:927
  93.1 52.2 %collective-permute-start.6 = (bf16[1024,1024]{1,0:T(8,128)(2,1)}, bf16[1024,1024]{1,0:T(8,128)(2,1)}, u32[]{:S(2)}, u32[]{:S(2)}) collective-permute-start(bf16[1024,1024]{1,0:T(8,128)(2,1)} %get-tuple-element.74), channel_id=1, source_target_pairs={{0,1},{1,0},{2,3},{3,2},{4,5},{5,4},{6,7},{7,6},{8,9},{9,8},{10,11... | collective-permute-start | bytes 6291464 | tf_op jit(solution)/shard_map/ppermute | solution.py:927
  93.4 96.8 %collective-permute-start.8 = (bf16[1024,1024]{1,0:T(8,128)(2,1)}, bf16[1024,1024]{1,0:T(8,128)(2,1)}, u32[]{:S(2)}, u32[]{:S(2)}) collective-permute-start(bf16[1024,1024]{1,0:T(8,128)(2,1)} %get-tuple-element.76), channel_id=1, source_target_pairs={{0,1},{1,0},{2,3},{3,2},{4,5},{5,4},{6,7},{7,6},{8,9},{9,8},{10,11... | collective-permute-start | bytes 6291464 | tf_op jit(solution)/shard_map/ppermute | solution.py:927
  115.1 76.7 %copy-start.1 = (s32[2]{0:T(128)S(1)}, s32[2]{0:T(128)}, u32[]{:S(2)}) copy-start(s32[2]{0:T(128)} %copy-done) | copy-start | bytes 28
  115.1 77.3 %copy-start.11 = (bf16[2,8,512]{2,1,0:T(8,128)(2,1)S(1)}, bf16[2,8,512]{2,1,0:T(8,128)(2,1)}, u32[]{:S(2)}) copy-start(bf16[2,8,512]{2,1,0:T(8,128)(2,1)} %maximum_select_fusion.3.refs_4_) | copy-start | bytes 49156
  115.2 77.3 %copy-start.12 = (bf16[2,8,512]{2,1,0:T(8,128)(2,1)S(1)}, bf16[2,8,512]{2,1,0:T(8,128)(2,1)}, u32[]{:S(2)}) copy-start(bf16[2,8,512]{2,1,0:T(8,128)(2,1)} %get-tuple-element.142.refs_4_) | copy-start | bytes 49156
  145.2 65.7 %collective-permute-start.7 = (bf16[1024,1024]{1,0:T(8,128)(2,1)}, bf16[1024,1024]{1,0:T(8,128)(2,1)}, u32[]{:S(2)}, u32[]{:S(2)}) collective-permute-start(bf16[1024,1024]{1,0:T(8,128)(2,1)} %collective-permute-done.6.up_near), channel_id=1, source_target_pairs={{0,2},{2,0},{4,6},{6,4},{8,10},{10,8},{12,14},{14,12},{16,18},{18,... | collective-permute-start | bytes 6291464 | tf_op jit(solution)/shard_map/ppermute | solution.py:935
  190.2 20.8 %collective-permute-start.9 = (bf16[1024,1024]{1,0:T(8,128)(2,1)}, bf16[1024,1024]{1,0:T(8,128)(2,1)}, u32[]{:S(2)}, u32[]{:S(2)}) collective-permute-start(bf16[1024,1024]{1,0:T(8,128)(2,1)} %collective-permute-done.8.down_near), channel_id=1, source_target_pairs={{0,2},{2,0},{4,6},{6,4},{8,10},{10,8},{12,14},{14,12},{16,18},{18,... | collective-permute-start | bytes 6291464 | tf_op jit(solution)/shard_map/ppermute | solution.py:935
  194.1 13.6 %collective-permute-start.4 = (bf16[256,1024]{1,0:T(8,128)(2,1)S(1)}, bf16[256,1024]{1,0:T(8,128)(2,1)}, u32[]{:S(2)}, u32[]{:S(2)}) collective-permute-start(bf16[256,1024]{1,0:T(8,128)(2,1)S(1)} %constant_dynamic-slice_fusion.5), channel_id=1, source_target_pairs={{0,1},{1,0},{2,3},{3,2},{4,5},{5,4},{6,7},{7,6},{8,9},{9,8},{10,11... | collective-permute-start | bytes 1572872 | tf_op jit(solution)/shard_map/ppermute | solution.py:927
  207.8 3.2 collective-permute-start.5
  278.1 123.8 %collective-permute-start.12 = (bf16[512,512]{1,0:T(8,128)(2,1)S(1)}, bf16[512,512]{1,0:T(8,128)(2,1)S(1)}, u32[]{:S(2)}, u32[]{:S(2)}) collective-permute-start(bf16[512,512]{1,0:T(8,128)(2,1)S(1)} %maximum_select_fusion.2), channel_id=1, source_target_pairs={{0,1},{1,0},{2,3},{3,2},{4,5},{5,4},{6,7},{7,6},{8,9},{9,8},{10,11... | collective-permute-start | bytes 1572872 | tf_op jit(solution)/shard_map/ppermute | solution.py:927
  429.9 51.6 %collective-permute-start.13 = (bf16[3,512,512]{2,1,0:T(8,128)(2,1)}, bf16[3,512,512]{2,1,0:T(8,128)(2,1)}, u32[]{:S(2)}, u32[]{:S(2)}) collective-permute-start(bf16[3,512,512]{2,1,0:T(8,128)(2,1)} %maximum_select_fusion), channel_id=1, source_target_pairs={{0,1},{1,0},{2,3},{3,2},{4,5},{5,4},{6,7},{7,6},{8,9},{9,8},{10,11... | collective-permute-start | bytes 4718600 | tf_op jit(solution)/shard_map/ppermute | solution.py:927
  436.8 169.1 %collective-permute-start.14 = (bf16[1024,1024]{1,0:T(8,128)(2,1)}, bf16[1024,1024]{1,0:T(8,128)(2,1)}, u32[]{:S(2)}, u32[]{:S(2)}) collective-permute-start(bf16[1024,1024]{1,0:T(8,128)(2,1)} %get-tuple-element.92), channel_id=1, source_target_pairs={{0,1},{1,0},{2,3},{3,2},{4,5},{5,4},{6,7},{7,6},{8,9},{9,8},{10,11... | collective-permute-start | bytes 6291464 | tf_op jit(solution)/shard_map/ppermute | solution.py:927
  468.9 229.8 %collective-permute-start.16 = (bf16[1024,1024]{1,0:T(8,128)(2,1)}, bf16[1024,1024]{1,0:T(8,128)(2,1)}, u32[]{:S(2)}, u32[]{:S(2)}) collective-permute-start(bf16[1024,1024]{1,0:T(8,128)(2,1)} %get-tuple-element.106), channel_id=1, source_target_pairs={{0,1},{1,0},{2,3},{3,2},{4,5},{5,4},{6,7},{7,6},{8,9},{9,8},{10,11... | collective-permute-start | bytes 6291464 | tf_op jit(solution)/shard_map/ppermute | solution.py:927
  471.6 129.9 %collective-permute-start.10 = (bf16[1024,1024]{1,0:T(8,128)(2,1)}, bf16[1024,1024]{1,0:T(8,128)(2,1)}, u32[]{:S(2)}, u32[]{:S(2)}) collective-permute-start(bf16[1024,1024]{1,0:T(8,128)(2,1)} %get-tuple-element.78), channel_id=1, source_target_pairs={{0,1},{1,0},{2,3},{3,2},{4,5},{5,4},{6,7},{7,6},{8,9},{9,8},{10,11... | collective-permute-start | bytes 6291464 | tf_op jit(solution)/shard_map/ppermute | solution.py:927
  471.7 221.7 %collective-permute-start.11 = (bf16[1536,1024]{1,0:T(8,128)(2,1)S(1)}, bf16[1536,1024]{1,0:T(8,128)(2,1)}, u32[]{:S(2)}, u32[]{:S(2)}) collective-permute-start(bf16[1536,1024]{1,0:T(8,128)(2,1)S(1)} %copy-done.2), channel_id=1, source_target_pairs={{0,1},{1,0},{2,3},{3,2},{4,5},{5,4},{6,7},{7,6},{8,9},{9,8},{10,11... | collective-permute-start | bytes 9437192 | tf_op jit(solution)/shard_map/ppermute | solution.py:927
  499.9 1.3 collective-permute-start.17
  501.2 22.4 %collective-permute-start.18 = (f32[24,1024]{1,0:T(8,128)S(1)}, f32[24,1024]{1,0:T(8,128)S(1)}, u32[]{:S(2)}, u32[]{:S(2)}) collective-permute-start(f32[24,1024]{1,0:T(8,128)S(1)} %fusion.15), channel_id=1, source_target_pairs={{0,4},{2,6},{4,0},{6,2},{8,12},{10,14},{12,8},{14,10},{16,20},{18,... | collective-permute-start | bytes 294920 | tf_op jit(solution)/shard_map/ppermute | solution.py:960
  523.6 4.0 collective-permute-start.19
  527.6 163.4 %collective-permute-start.15 = (bf16[512,1024]{1,0:T(8,128)(2,1)}, bf16[512,1024]{1,0:T(8,128)(2,1)}, u32[]{:S(2)}, u32[]{:S(2)}) collective-permute-start(bf16[512,1024]{1,0:T(8,128)(2,1)} %get-tuple-element.99), channel_id=1, source_target_pairs={{0,1},{1,0},{2,3},{3,2},{4,5},{5,4},{6,7},{7,6},{8,9},{9,8},{10,11... | collective-permute-start | bytes 3145736 | tf_op jit(solution)/shard_map/ppermute | solution.py:927
  601.5 4.4 collective-permute-start.20
  604.6 85.1 %copy-start.8 = (f32[2,1024,4]{1,2,0:T(4,128)S(1)}, f32[2,1024,4]{1,2,0:T(4,128)}, u32[]{:S(2)}) copy-start(f32[2,1024,4]{1,2,0:T(4,128)} %param.34) | copy-start | bytes 98308
  604.6 85.1 %copy-start.13 = (f32[2,1024,4]{1,2,0:T(4,128)S(1)}, f32[2,1024,4]{1,2,0:T(4,128)}, u32[]{:S(2)}) copy-start(f32[2,1024,4]{1,2,0:T(4,128)} %param.36) | copy-start | bytes 98308
  604.6 85.1 %copy-start.14 = (f32[2,1024,4]{1,2,0:T(4,128)S(1)}, f32[2,1024,4]{1,2,0:T(4,128)}, u32[]{:S(2)}) copy-start(f32[2,1024,4]{1,2,0:T(4,128)} %param.38) | copy-start | bytes 98308
  604.6 85.8 %copy-start.10 = (f32[2,4,1024]{2,1,0:T(4,128)S(1)}, f32[2,4,1024]{2,1,0:T(4,128)}, u32[]{:S(2)}) copy-start(f32[2,4,1024]{2,1,0:T(4,128)} %param.35) | copy-start | bytes 98308
  604.6 85.8 %copy-start.15 = (f32[2,4,1024]{2,1,0:T(4,128)S(1)}, f32[2,4,1024]{2,1,0:T(4,128)}, u32[]{:S(2)}) copy-start(f32[2,4,1024]{2,1,0:T(4,128)} %param.37) | copy-start | bytes 98308
  604.6 85.8 %copy-start.16 = (f32[2,4,1024]{2,1,0:T(4,128)S(1)}, f32[2,4,1024]{2,1,0:T(4,128)}, u32[]{:S(2)}) copy-start(f32[2,4,1024]{2,1,0:T(4,128)} %param.39) | copy-start | bytes 98308
  605.9 82.6 %collective-permute-start.21 = (f32[24,1024]{1,0:T(8,128)S(1)}, f32[24,1024]{1,0:T(8,128)S(1)}, u32[]{:S(2)}, u32[]{:S(2)}) collective-permute-start(f32[24,1024]{1,0:T(8,128)S(1)} %add.311), channel_id=1, source_target_pairs={{0,1},{1,0},{2,3},{3,2},{4,5},{5,4},{6,7},{7,6},{8,9},{9,8},{10,11... | collective-permute-start | bytes 294920 | tf_op jit(solution)/shard_map/ppermute | solution.py:927
  (19 other events, 403.0 us)

commit v2 on v1

--- a/solution.py
+++ b/solution.py
@@ -566,6 +566,7 @@
     down_near,
     down_far,
     block_ref,
+    full_ref,
     resid_grad_ref,
     own_grad_ref,
     far_grad_ref,
@@ -630,9 +631,9 @@
         return carry
 
     def finish():
-        block_ref[...] = (residual_ref[...] + acc_ref[...] + down_bias_ref[...]).astype(
-            block_ref.dtype
-        )
+        block = (residual_ref[...] + acc_ref[...] + down_bias_ref[...]).astype(block_ref.dtype)
+        block_ref[...] = block
+        full_ref[...] = block
 
     @pl.when(live > 0)
     def _():
@@ -676,8 +677,12 @@
 UNROLL = 2
 
 
+def without(kernel, place, *refs):
+    return kernel(*refs[:place], *refs[place + 1 :])
+
+
 def middle(
-    table, tokens, cotangent, own, far, out_bias, gain, shift, up_bias, down_bias, weights
+    table, tokens, cotangent, own, far, out_bias, gain, shift, up_bias, down_bias, weights, into
 ):
     rows, width = table.shape[1] * MID_ROWS, tokens.shape[1]
     columns = far.shape[1]
@@ -690,8 +695,26 @@
     low = jax.ShapeDtypeStruct((rows, width), jnp.bfloat16)
     thin = jax.ShapeDtypeStruct((rows, columns), jnp.bfloat16)
     wide = pltpu.VMEM((MID_ROWS, width), jnp.float32)
+    operands = (
+        table,
+        tokens,
+        cotangent,
+        own,
+        far,
+        out_bias,
+        gain,
+        shift,
+        up_bias,
+        down_bias,
+        *weights,
+    )
+    place = len(operands)
+    kernel, extra, aliases = middle_kernel, (), {}
+    if into is not None:
+        kernel = functools.partial(without, middle_kernel, place)
+        extra, aliases = (into,), {place: 1}
     return pl.pallas_call(
-        middle_kernel,
+        kernel,
         grid_spec=pltpu.PrefetchScalarGridSpec(
             num_scalar_prefetch=1,
             grid=(rows // MID_ROWS,),
@@ -699,8 +722,8 @@
             + [pl.BlockSpec((MID_ROWS, columns), lambda i, t, a=a: (t[a, i], 0)) for a in (1, 3)]
             + [vector] * 3
             + [pl.BlockSpec(up_bias.shape, lambda i, t: (0, 0, 0)), vector]
-            + [pl.BlockSpec(memory_space=pl.ANY)] * 9,
-            out_specs=[tile, tile, part, part],
+            + [pl.BlockSpec(memory_space=pl.ANY)] * (9 + len(extra)),
+            out_specs=[tile, picked, tile, part, part],
             scratch_shapes=[
                 pltpu.VMEM((width, width), jnp.bfloat16),
                 pltpu.VMEM((chunks, width, CHUNK), jnp.bfloat16),
@@ -713,7 +736,8 @@
                 pltpu.SemaphoreType.DMA((3 + 2 * chunks,)),
             ],
         ),
-        out_shape=[low, low, thin, thin],
+        out_shape=[low, jax.ShapeDtypeStruct(tokens.shape, jnp.bfloat16), low, thin, thin],
+        input_output_aliases=aliases,
         compiler_params=pltpu.CompilerParams(vmem_limit_bytes=56 << 20),
         cost_estimate=pl.CostEstimate(
             flops=rows * width * (units * 8 + width * 4),
@@ -721,19 +745,7 @@
             transcendentals=rows * units,
         ),
         name="middle",
-    )(
-        table,
-        tokens,
-        cotangent,
-        own,
-        far,
-        out_bias,
-        gain,
-        shift,
-        up_bias,
-        down_bias,
-        *weights,
-    )
+    )(*operands, *extra)
 
 
 PROJECT_ROWS = 256
@@ -832,6 +844,7 @@
     near_ref,
     far_ref,
     input_ref,
+    full_ref,
     down_grad_ref,
     query_up_ref,
     value_up_ref,
@@ -849,41 +862,52 @@
         query_up_ref[...] = jnp.zeros_like(query_up_ref)
         value_up_ref[...] = jnp.zeros_like(value_up_ref)
 
-    normal, inverse = centred(tokens_ref[...].astype(jnp.float32))
-    normed = (normal * gain_ref[...] + shift_ref[...]).astype(jnp.bfloat16)
-    query = jnp.concatenate((query_own[...], query_far[...]), axis=1)
-    key = jnp.concatenate((key_own[...], key_far[...]), axis=1)
-    value = jnp.concatenate((value_own[...], value_far[...]), axis=1)
-    adapter = 8.0 * (dot_t(query, up_ref[0]) + dot_t(value, up_ref[1]))
-    high = adapter.astype(jnp.bfloat16)
-    rest = (adapter - high.astype(jnp.float32)).astype(jnp.bfloat16)
-    down_grad_ref[...] += dot(high.astype(jnp.float32).T.astype(jnp.bfloat16), normed) + dot(
-        rest.astype(jnp.float32).T.astype(jnp.bfloat16), normed
-    )
-    low = low_ref[...].astype(jnp.bfloat16)
-    query_up_ref[...] += dot(low, query)
-    value_up_ref[...] += dot(low, value)
-
     @pl.when(first)
     def _():
         for load in loads:
             load.wait()
 
-    grad = (
-        dot_t(query, weight_ref[0])
-        + dot_t(key, weight_ref[1])
-        + dot_t(value, weight_ref[2])
-        + dot(high, down_ref[...])
-        + dot(rest, down_ref[...])
-    )
-    input_ref[...] = (
-        resid_grad_ref[...].astype(jnp.float32)
-        + norm_backward(grad, gain_ref[...], normal, inverse)
-    ).astype(input_ref.dtype)
+    live = table_ref[4, pl.program_id(0)]
+
+    @pl.when(live > 0)
+    def _():
+        normal, inverse = centred(tokens_ref[...].astype(jnp.float32))
+        normed = (normal * gain_ref[...] + shift_ref[...]).astype(jnp.bfloat16)
+        query = jnp.concatenate((query_own[...], query_far[...]), axis=1)
+        key = jnp.concatenate((key_own[...], key_far[...]), axis=1)
+        value = jnp.concatenate((value_own[...], value_far[...]), axis=1)
+        adapter = 8.0 * (dot_t(query, up_ref[0]) + dot_t(value, up_ref[1]))
+        high = adapter.astype(jnp.bfloat16)
+        rest = (adapter - high.astype(jnp.float32)).astype(jnp.bfloat16)
+        down_grad_ref[...] += dot(high.astype(jnp.float32).T.astype(jnp.bfloat16), normed) + dot(
+            rest.astype(jnp.float32).T.astype(jnp.bfloat16), normed
+        )
+        low = low_ref[...].astype(jnp.bfloat16)
+        query_up_ref[...] += dot(low, query)
+        value_up_ref[...] += dot(low, value)
+
+        grad = (
+            dot_t(query, weight_ref[0])
+            + dot_t(key, weight_ref[1])
+            + dot_t(value, weight_ref[2])
+            + dot(high, down_ref[...])
+            + dot(rest, down_ref[...])
+        )
+        result = (
+            resid_grad_ref[...].astype(jnp.float32)
+            + norm_backward(grad, gain_ref[...], normal, inverse)
+        ).astype(input_ref.dtype)
+        input_ref[...] = result
+        full_ref[...] = result
+
+    @pl.when(live <= 0)
+    def _():
+        input_ref[...] = jnp.zeros_like(input_ref)
+        full_ref[...] = jnp.zeros_like(full_ref)
 
 
 def first_backward(
-    table, tokens, resid_grad, low, own, far, gain, shift, down, up, weights
+    table, tokens, resid_grad, low, own, far, gain, shift, down, up, weights, into
 ):
     tiles = table.shape[1]
     rows, width = tiles * PROJECT_ROWS, tokens.shape[1]
@@ -893,8 +917,14 @@
     vector = pl.BlockSpec((1, width), lambda i, t: (0, 0))
     small = pl.BlockSpec((pairs, width), lambda i, t: (0, 0))
     sums = jax.ShapeDtypeStruct((pairs, width), jnp.float32)
+    operands = (table, tokens, resid_grad, low, *own, *far, gain, shift, down, up, *weights)
+    place = len(operands)
+    kernel, extra, aliases = first_backward_kernel, (), {}
+    if into is not None:
+        kernel = functools.partial(without, first_backward_kernel, place)
+        extra, aliases = (into,), {place: 1}
     return pl.pallas_call(
-        first_backward_kernel,
+        kernel,
         grid_spec=pltpu.PrefetchScalarGridSpec(
             num_scalar_prefetch=1,
             grid=(tiles,),
@@ -906,21 +936,26 @@
             + [pl.BlockSpec((PROJECT_ROWS, columns), lambda i, t: (t[3, i], 0))] * 3
             + [pl.BlockSpec((PROJECT_ROWS, columns), lambda i, t: (i, 0))] * 3
             + [vector, vector, small, pl.BlockSpec(up.shape, lambda i, t: (0, 0, 0))]
-            + [pl.BlockSpec(memory_space=pl.ANY)] * 3,
-            out_specs=[pl.BlockSpec((PROJECT_ROWS, width), lambda i, t: (i, 0))] + [small] * 3,
+            + [pl.BlockSpec(memory_space=pl.ANY)] * (3 + len(extra)),
+            out_specs=[pl.BlockSpec((PROJECT_ROWS, width), lambda i, t: (i, 0)), tile] + [small] * 3,
             scratch_shapes=[
                 pltpu.VMEM((3, width, width), jnp.bfloat16),
                 pltpu.SemaphoreType.DMA((3,)),
             ],
         ),
-        out_shape=[jax.ShapeDtypeStruct((rows, width), jnp.bfloat16)] + [sums] * 3,
+        out_shape=[
+            jax.ShapeDtypeStruct((rows, width), jnp.bfloat16),
+            jax.ShapeDtypeStruct(tokens.shape, jnp.bfloat16),
+        ]
+        + [sums] * 3,
+        input_output_aliases=aliases,
         cost_estimate=pl.CostEstimate(
             flops=rows * width * width * 7,
             bytes_accessed=rows * width * 12 + 6 * width * width,
             transcendentals=rows,
         ),
         name="first_backward",
-    )(table, tokens, resid_grad, low, *own, *far, gain, shift, down, up, *weights)
+    )(*operands, *extra)
 
 
 def swap(value):
@@ -1128,7 +1163,7 @@
         (token_table, own_table, live_table, jnp.arange(token_table.shape[0], dtype=jnp.int32))
     )
 
-    def run_middle(first, last):
+    def run_middle(first, last, into):
         return middle(
             middle_table[:, first:last],
             flat_tokens,
@@ -1141,11 +1176,14 @@
             up_bias,
             row(feedforward_down_bias),
             weights,
+            into,
         )
 
-    block_zero, resid_zero, *grads_zero = run_middle(0, tiles)
+    block_zero, block_out, resid_zero, *grads_zero = run_middle(0, tiles, None)
     block_zero_got = swap(block_zero)
-    block_rest, resid_rest, *grads_rest = run_middle(tiles, token_table.shape[0])
+    block_rest, block_out, resid_rest, *grads_rest = run_middle(
+        tiles, token_table.shape[0], block_out
+    )
     grad_got = swap(core_order(grads_rest[1][length:], 1))
     block_rest_got = swap(block_rest)
     grad_kept = grads_rest[0][length:]
@@ -1164,7 +1202,7 @@
 
     span = jnp.arange(tiles, dtype=jnp.int32)
 
-    def back_first(own, far, table, resid_grad):
+    def back_first(own, far, table, resid_grad, into):
         return first_backward(
             table,
             flat_tokens,
@@ -1177,6 +1215,7 @@
             down_low,
             up_both,
             qkv,
+            into,
         )
 
     def whole_rows(index):
@@ -1189,7 +1228,7 @@
         [lax.dynamic_slice_in_dim(p[0], (1 - me) * half, half, 0) for p in split_own]
     )
     split_got = swap(core_order(split_sent, 2))
-    first_zero = back_first(*back_zero, whole_rows(0), resid_zero)
+    first_zero = back_first(*back_zero, whole_rows(0), resid_zero, None)
     send_zero = swap(first_zero[0])
     back_one = back_whole(1, grads_rest)
     first_split = back_first(
@@ -1205,13 +1244,14 @@
             )
         ),
         resid_rest,
+        first_zero[1],
     )
     send_split = swap(first_split[0])
-    first_one = back_first(*back_one, whole_rows(1), resid_rest)
+    first_one = back_first(*back_one, whole_rows(1), resid_rest, first_split[1])
     send_one = swap(first_one[0])
 
     down_sum, query_sum, value_sum = (
-        first_zero[i] + first_split[i] + first_one[i] for i in range(1, 4)
+        first_zero[i] + first_split[i] + first_one[i] for i in range(2, 5)
     )
     up_sum = 8.0 * jnp.concatenate((query_sum[:rank], value_sum[rank:]))
     up_mine = up_sum[:, :columns]
@@ -1225,33 +1265,28 @@
     grad_down = total[: 2 * rank].reshape(2, rank, width).transpose(0, 2, 1) / active
     grad_up = total[2 * rank : 4 * rank].reshape(2, rank, width) / active
 
-    def place(pieces):
-        out = jnp.zeros((seqs * length, width), bf16)
+    there = split * length + half * (1 - me)
+
+    def fill(out, pieces):
         for piece, start in pieces:
             out = lax.dynamic_update_slice_in_dim(out, piece, start, 0)
         return out.reshape(tokens.shape)
 
-    here = split * length + half * me
-    there = split * length + half * (1 - me)
-    block_out = place(
+    block_out = fill(
+        block_out,
         (
-            (block_zero, mine[0] * length),
-            (block_rest[:length], mine[1] * length),
-            (block_rest[length:], here),
             (block_zero_got, theirs[0] * length),
             (block_rest_got[:length], theirs[1] * length),
             (block_rest_got[length:], there),
-        )
-    )
-    input_grad = place(
+        ),
+    )
+    input_grad = fill(
+        first_one[1],
         (
-            (first_zero[0], mine[0] * length),
-            (first_split[0], here),
-            (first_one[0], mine[1] * length),
             (send_zero, theirs[0] * length),
             (send_split, there),
             (send_one, theirs[1] * length),
-        )
+        ),
     )
     new_down = adam_decay_update(
         adapter_down_factor, grad_down, down_first_moment, down_second_moment

time: 711 us -> 636 us (0.89)
  the two profiles are of different devices: /device:TPU:1 before, /device:TPU:28 now
where the time goes in v2:
time: 636 us; the launch traced here: 626 us
  Pallas kernels  360 us (57%)
  waiting for transfers between devices  143 us (22%)
  starting transfers between devices  51.8 us (8%)
  local copies, waits for them, and re-layouts  42.2 us (7%)
  other arithmetic  21 us (3%)
  between operations  9.28 us (1%)
    ppermute x14, waiting for transfers between devices, swap(): return lax.ppermute(value, 'mp', [(0, 1), (1, 0)])  129 us
    pallas_call x2, Pallas kernels, middle(): pl.pallas_call(kernel, grid_spec=pltpu.PrefetchScalarGridSpec(num_scalar_...  122 us
    pallas_call x5, Pallas kernels, attention_backward(): pl.pallas_call(attention_backward_kernel, grid_spec=pltpu.PrefetchScalarG...  75.4 us
    pallas_call x2, Pallas kernels, attention_forward(): pl.pallas_call(attention_forward_kernel, grid_spec=pltpu.PrefetchScalarGr...  66.9 us
    pallas_call x3, Pallas kernels, first_backward(): pl.pallas_call(kernel, grid_spec=pltpu.PrefetchScalarGridSpec(num_scalar_...  49.5 us
    pallas_call x2, Pallas kernels, project(): pl.pallas_call(functools.partial(project_kernel, len(weights)), grid_spec...  46.3 us
    ppermute x4, starting transfers between devices, sum_all(): lax.ppermute(value, 'dp', [(i, i ^ bit) for i in range(count)])  24.6 us
    ppermute x4, starting transfers between devices, core_swap(): lax.ppermute(value, 'dp', [(i, i ^ 1) for i in range(lax.axis_size('dp'))])  15.4 us
  transfers between devices with their start and end apart: 22, of which 9 were waited for; matrix products, arithmetic and copies ran while one was open for 9% of the time, Pallas kernels for 38%

profile of v2, /device:TPU:28, one launch (start us, length us, event | category | flops | bytes accessed | tf_op | source)
XLA Modules:
  0.0 626.5 jit_solution(8807155330358800764)
XLA Ops:
  9.5 27.0 %project.2 = (bf16[3072,512]{1,0:T(8,128)(2,1)}, bf16[3072,512]{1,0:T(8,128)(2,1)}, bf16[3072,512]{1,0:T(8,128)(2,1)}, f32[8,3072]{1,0:T(8,128)}) custom-call(s32[12]{0:T(128)} %pad_add_fusion.5.table_ref, bf16[5120,1024]{1,0:T(8,128)(2,1)} %bitcast.86, f32[1,1024]{1,0:T(1,128)} %bitcast.119, f32[1,1024]{1,0:T(1,128)} %bitcast.124, ...), custom_call_target="tpu_custom_call" | custom-call | flops 9663676416 | bytes 18874368 | tf_op jit(solution)/shard_map/project/pallas_call | solution.py:798
  41.0 40.3 %attention_forward.2 = (bf16[3,1024,512]{2,1,0:T(8,128)(2,1)}, f32[3,4,2,1024]{3,2,1,0:T(2,128)}) custom-call(s32[3]{0:T(128)} %pad_add_fusion.4.lens_ref, bf16[3,1024,512]{2,1,0:T(8,128)(2,1)} %bitcast.96, bf16[3,1024,512]{2,1,0:T(8,128)(2,1)} %bitcast.100, bf16[3,1024,512]{2,1,0:T(8,128)(2,1)} %bitcast.104), custom_call_target="tpu_custom_call" | custom-call | flops 4831838208 | bytes 12582912 | tf_op jit(solution)/shard_map/attention_forward/pallas_call | solution.py:381
  81.3 2.3 slice.132
  84.7 4.8 constant_dynamic-slice_fusion.3
  96.5 19.3 %project.3 = (bf16[2048,512]{1,0:T(8,128)(2,1)}, bf16[2048,512]{1,0:T(8,128)(2,1)}, bf16[2048,512]{1,0:T(8,128)(2,1)}, f32[8,2048]{1,0:T(8,128)}) custom-call(s32[8]{0:T(128)} %copy-done.26, bf16[5120,1024]{1,0:T(8,128)(2,1)} %bitcast.87, f32[1,1024]{1,0:T(1,128)} %bitcast.120, f32[1,1024]{1,0:T(1,128)} %bitcast.125, ...), custom_call_target="tpu_custom_call" | custom-call | flops 6442450944 | bytes 13631488 | tf_op jit(solution)/shard_map/project/pallas_call | solution.py:798
  115.8 26.6 %attention_forward.3 = (bf16[2,1024,512]{2,1,0:T(8,128)(2,1)}, f32[2,4,2,1024]{3,2,1,0:T(2,128)}) custom-call(s32[2]{0:T(128)} %copy-done, bf16[2,1024,512]{2,1,0:T(8,128)(2,1)} %bitcast.146, bf16[2,1024,512]{2,1,0:T(8,128)(2,1)} %bitcast.149, bf16[2,1024,512]{2,1,0:T(8,128)(2,1)} %bitcast.152), custom_call_target="tpu_custom_call" | custom-call | flops 3221225472 | bytes 8388608 | tf_op jit(solution)/shard_map/attention_forward/pallas_call | solution.py:381
  142.4 6.6 %collective-permute-start.7 = (bf16[1024,1024]{1,0:T(8,128)(2,1)}, bf16[1024,1024]{1,0:T(8,128)(2,1)}, u32[]{:S(2)}, u32[]{:S(2)}) collective-permute-start(bf16[1024,1024]{1,0:T(8,128)(2,1)} %collective-permute-done.6.up_near.refs_14_), channel_id=1, source_target_pairs={{0,2},{2,0},{4,6},{6,4},{8,10},{10,8},{12,14},{14,12},{16,18},{18,... | collective-permute-start | bytes 6291464 | tf_op jit(solution)/shard_map/ppermute | solution.py:970
  149.0 31.2 %collective-permute-done.8.down_near.refs_17_ = bf16[1024,1024]{1,0:T(8,128)(2,1)} collective-permute-done((bf16[1024,1024]{1,0:T(8,128)(2,1)}, bf16[1024,1024]{1,0:T(8,128)(2,1)}, u32[]{:S(2)}, u32[]{:S(2)}) %collective-permute-start.8) | collective-permute-done | bytes 2097184 | tf_op jit(solution)/shard_map/ppermute | solution.py:962
  180.2 6.3 %collective-permute-start.9 = (bf16[1024,1024]{1,0:T(8,128)(2,1)}, bf16[1024,1024]{1,0:T(8,128)(2,1)}, u32[]{:S(2)}, u32[]{:S(2)}) collective-permute-start(bf16[1024,1024]{1,0:T(8,128)(2,1)} %collective-permute-done.8.down_near.refs_17_), channel_id=1, source_target_pairs={{0,2},{2,0},{4,6},{6,4},{8,10},{10,8},{12,14},{14,12},{16,18},{18,... | collective-permute-start | bytes 6291464 | tf_op jit(solution)/shard_map/ppermute | solution.py:970
  195.2 8.1 %collective-permute-done.4.out_near.refs_11_ = bf16[256,1024]{1,0:T(8,128)(2,1)} collective-permute-done((bf16[256,1024]{1,0:T(8,128)(2,1)S(1)}, bf16[256,1024]{1,0:T(8,128)(2,1)}, u32[]{:S(2)}, u32[]{:S(2)}) %collective-permute-start.4) | collective-permute-done | bytes 524320 | tf_op jit(solution)/shard_map/ppermute | solution.py:962
  203.3 2.4 collective-permute-start.5
  206.4 2.7 pad_maximum_fusion.attended_far.refs_4_
  209.9 56.8 %middle.2 = (bf16[1024,1024]{1,0:T(8,128)(2,1)}, bf16[5120,1024]{1,0:T(8,128)(2,1)}, bf16[1024,1024]{1,0:T(8,128)(2,1)}, bf16[1024,512]{1,0:T(8,128)(2,1)}, bf16[1024,512]{1,0:T(8,128)(2,1)}) custom-call(s32[4,4]{1,0:T(4,128)} %bitcast.129, bf16[5120,1024]{1,0:T(8,128)(2,1)} %bitcast.88, bf16[5120,1024]{1,0:T(8,128)(2,1)} %bitcast.135, ...), custom_call_target="tpu_custom_call" | custom-call | flops 38654705664 | bytes 29360128 | tf_op jit(solution)/shard_map/middle/pallas_call | solution.py:716
  266.7 64.8 %middle.3 = (bf16[1536,1024]{1,0:T(8,128)(2,1)}, bf16[5120,1024]{1,0:T(8,128)(2,1)}, bf16[1536,1024]{1,0:T(8,128)(2,1)}, bf16[1536,512]{1,0:T(8,128)(2,1)}, bf16[1536,512]{1,0:T(8,128)(2,1)}) custom-call(s32[4,6]{1,0:T(4,128)} %slice.127.refs_0_, bf16[5120,1024]{1,0:T(8,128)(2,1)} %bitcast.89, ...), custom_call_target="tpu_custom_call", output_to_operand_aliasing={{1}: (19, {})} | custom-call | flops 57982058496 | bytes 35651584 | tf_op jit(solution)/shard_map/middle/pallas_call | solution.py:716
  338.4 20.5 %attention_backward.8 = (bf16[1,1024,512]{2,1,0:T(8,128)(2,1)}, bf16[1,1024,512]{2,1,0:T(8,128)(2,1)}, bf16[1,1024,512]{2,1,0:T(8,128)(2,1)}) custom-call(s32[1]{0:T(128)} %get-tuple-element.159.lens_ref, bf16[3,1024,512]{2,1,0:T(8,128)(2,1)} %bitcast.97, bf16[3,1024,512]{2,1,0:T(8,128)(2,1)} %bitcast.101, bf16[3,1024,512]{2,1,0:T(8,128)(2,1)} %bitcast.105, ...), custom_call_target="tpu_custom_call" | custom-call | flops 3758096384 | bytes 7340032 | tf_op jit(solution)/shard_map/attention_backward/pallas_call | solution.py:491
  361.2 20.3 %attention_backward.7 = (bf16[1,1024,512]{2,1,0:T(8,128)(2,1)}, bf16[1,1024,512]{2,1,0:T(8,128)(2,1)}, bf16[1,1024,512]{2,1,0:T(8,128)(2,1)}) custom-call(s32[1]{0:T(128)} %bitcast.13.lens_ref, bf16[3,1024,512]{2,1,0:T(8,128)(2,1)} %bitcast.98, bf16[3,1024,512]{2,1,0:T(8,128)(2,1)} %bitcast.102, bf16[3,1024,512]{2,1,0:T(8,128)(2,1)} %bitcast.106, ...), custom_call_target="tpu_custom_call" | custom-call | flops 3758096384 | bytes 7340032 | tf_op jit(solution)/shard_map/attention_backward/pallas_call | solution.py:491
  388.0 20.6 %attention_backward.9 = (bf16[1,1024,512]{2,1,0:T(8,128)(2,1)}, bf16[1,1024,512]{2,1,0:T(8,128)(2,1)}, bf16[1,1024,512]{2,1,0:T(8,128)(2,1)}) custom-call(s32[1]{0:T(128)} %get-tuple-element.159.lens_ref, bf16[2,1024,512]{2,1,0:T(8,128)(2,1)} %bitcast.147, bf16[2,1024,512]{2,1,0:T(8,128)(2,1)} %bitcast.150, bf16[2,1024,512]{2,1,0:T(8,128)(2,1)} %bitcast.153, ...), custom_call_target="tpu_custom_call" | custom-call | flops 3758096384 | bytes 7340032 | tf_op jit(solution)/shard_map/attention_backward/pallas_call | solution.py:491
  408.6 21.7 %first_backward.3 = (bf16[1024,1024]{1,0:T(8,128)(2,1)}, bf16[5120,1024]{1,0:T(8,128)(2,1)}, f32[8,1024]{1,0:T(8,128)}, f32[8,1024]{1,0:T(8,128)}, f32[8,1024]{1,0:T(8,128)}) custom-call(s32[5,4]{1,0:T(8,128)} %stack.86.table_ref, bf16[5120,1024]{1,0:T(8,128)(2,1)} %bitcast.90, bf16[1024,1024]{1,0:T(8,128)(2,1)} %get-tuple-element.102.resid_grad_ref, ...), custom_call_target="tpu_custom_call" | custom-call | flops 7516192768 | bytes 18874368 | tf_op jit(solution)/shard_map/first_backward/pallas_call | solution.py:926
  431.0 6.9 %attention_backward.5 = (bf16[1,1024,512]{2,1,0:T(8,128)(2,1)}, bf16[1,1024,512]{2,1,0:T(8,128)(2,1)}, bf16[1,1024,512]{2,1,0:T(8,128)(2,1)}) custom-call(s32[1]{0:T(128)} %get-tuple-element.160.lens_ref, bf16[3,1024,512]{2,1,0:T(8,128)(2,1)} %bitcast.99, bf16[3,1024,512]{2,1,0:T(8,128)(2,1)} %bitcast.103, bf16[3,1024,512]{2,1,0:T(8,128)(2,1)} %bitcast.107, ...), custom_call_target="tpu_custom_call" | custom-call | flops 3758096384 | bytes 7340032 | tf_op jit(solution)/shard_map/attention_backward/pallas_call | solution.py:491
  437.9 7.1 %attention_backward.6 = (bf16[1,1024,512]{2,1,0:T(8,128)(2,1)}, bf16[1,1024,512]{2,1,0:T(8,128)(2,1)}, bf16[1,1024,512]{2,1,0:T(8,128)(2,1)}) custom-call(s32[1]{0:T(128)} %get-tuple-element.160.lens_ref, bf16[2,1024,512]{2,1,0:T(8,128)(2,1)} %bitcast.148, bf16[2,1024,512]{2,1,0:T(8,128)(2,1)} %bitcast.151, bf16[2,1024,512]{2,1,0:T(8,128)(2,1)} %bitcast.154, ...), custom_call_target="tpu_custom_call" | custom-call | flops 3758096384 | bytes 7340032 | tf_op jit(solution)/shard_map/attention_backward/pallas_call | solution.py:491
  445.0 40.9 %collective-permute-done.13 = bf16[3,512,512]{2,1,0:T(8,128)(2,1)} collective-permute-done((bf16[3,512,512]{2,1,0:T(8,128)(2,1)}, bf16[3,512,512]{2,1,0:T(8,128)(2,1)}, u32[]{:S(2)}, u32[]{:S(2)}) %collective-permute-start.13) | collective-permute-done | bytes 1572896 | tf_op jit(solution)/shard_map/ppermute | solution.py:962
  485.9 2.5 slice_bitcast_fusion
  488.4 14.1 %first_backward.4 = (bf16[512,1024]{1,0:T(8,128)(2,1)}, bf16[5120,1024]{1,0:T(8,128)(2,1)}, f32[8,1024]{1,0:T(8,128)}, f32[8,1024]{1,0:T(8,128)}, f32[8,1024]{1,0:T(8,128)}) custom-call(s32[5,2]{1,0:T(8,128)} %copy.32.refs_0_, bf16[5120,1024]{1,0:T(8,128)(2,1)} %bitcast.91, ...), custom_call_target="tpu_custom_call", output_to_operand_aliasing={{1}: (17, {})} | custom-call | flops 3758096384 | bytes 12582912 | tf_op jit(solution)/shard_map/first_backward/pallas_call | solution.py:926
  502.6 13.7 %first_backward.5 = (bf16[1024,1024]{1,0:T(8,128)(2,1)}, bf16[5120,1024]{1,0:T(8,128)(2,1)}, f32[8,1024]{1,0:T(8,128)}, f32[8,1024]{1,0:T(8,128)}, f32[8,1024]{1,0:T(8,128)}) custom-call(s32[5,4]{1,0:T(8,128)} %stack.81.refs_0_, bf16[5120,1024]{1,0:T(8,128)(2,1)} %bitcast.92, ...), custom_call_target="tpu_custom_call", output_to_operand_aliasing={{1}: (17, {})} | custom-call | flops 7516192768 | bytes 18874368 | tf_op jit(solution)/shard_map/first_backward/pallas_call | solution.py:926
  518.8 24.3 %collective-permute-start.17 = (f32[24,1024]{1,0:T(8,128)S(1)}, f32[24,1024]{1,0:T(8,128)S(1)}, u32[]{:S(2)}, u32[]{:S(2)}) collective-permute-start(f32[24,1024]{1,0:T(8,128)S(1)} %maximum_maximum_fusion), channel_id=1, source_target_pairs={{0,2},{2,0},{4,6},{6,4},{8,10},{10,8},{12,14},{14,12},{16,18},{18,... | collective-permute-start | bytes 294920 | tf_op jit(solution)/shard_map/ppermute | solution.py:995
  544.2 5.0 collective-permute-done.18
  549.4 4.6 collective-permute-done.19
  557.9 3.1 constant_dynamic-update-slice_fusion.3
  561.0 2.9 collective-permute-done.20
  565.3 3.1 constant_dynamic-update-slice_fusion.2
  568.4 47.1 %collective-permute-done.21 = f32[24,1024]{1,0:T(8,128)S(1)} collective-permute-done((f32[24,1024]{1,0:T(8,128)S(1)}, f32[24,1024]{1,0:T(8,128)S(1)}, u32[]{:S(2)}, u32[]{:S(2)}) %collective-permute-start.21) | collective-permute-done | bytes 98336 | tf_op jit(solution)/shard_map/ppermute | solution.py:962
  623.0 3.1 constant_dynamic-update-slice_fusion
  (184 shorter events, 56.6 us)
Async XLA Ops:
  2.2 36.2 %collective-permute-start = (bf16[3,1024,256]{2,1,0:T(8,128)(2,1)S(1)}, bf16[3,1024,256]{2,1,0:T(8,128)(2,1)S(1)}, u32[]{:S(2)}, u32[]{:S(2)}) collective-permute-start(bf16[3,1024,256]{2,1,0:T(8,128)(2,1)S(1)} %constant_dynamic-slice_fusion.6), channel_id=1, source_target_pairs={{0,1},{1,0},{2,3},{3,2},{4,5},{5,4},{6,7},{7,6},{8,9},{9,8},{10,11... | collective-permute-start | bytes 4718600 | tf_op jit(solution)/shard_map/ppermute | solution.py:962
  38.4 42.9 %copy-start.2 = (bf16[3,1024,256]{2,1,0:T(8,128)(2,1)}, bf16[3,1024,256]{2,1,0:T(8,128)(2,1)S(1)}, u32[]{:S(2)}) copy-start(bf16[3,1024,256]{2,1,0:T(8,128)(2,1)S(1)} %collective-permute-done.refs_5_.near_ref.refs_15_) | copy-start | bytes 4718596
  38.4 51.6 %collective-permute-start.1 = (bf16[3,1024,256]{2,1,0:T(8,128)(2,1)S(1)}, bf16[3,1024,256]{2,1,0:T(8,128)(2,1)S(1)}, u32[]{:S(2)}, u32[]{:S(2)}) collective-permute-start(bf16[3,1024,256]{2,1,0:T(8,128)(2,1)S(1)} %collective-permute-done.refs_5_.near_ref.refs_15_), channel_id=1, source_target_pairs={{0,2},{2,0},{4,6},{6,4},{8,10},{10,8},{12,14},{14,12},{16,18},{18,... | collective-permute-start | bytes 4718600 | tf_op jit(solution)/shard_map/ppermute | solution.py:970
  39.8 54.7 %copy-start = (s32[2]{0:T(128)}, s32[2]{0:T(128)S(1)}, u32[]{:S(2)}) copy-start(s32[2]{0:T(128)S(1)} %fusion.7.lens_ref) | copy-start | bytes 28
  89.5 52.9 %collective-permute-start.6 = (bf16[1024,1024]{1,0:T(8,128)(2,1)}, bf16[1024,1024]{1,0:T(8,128)(2,1)}, u32[]{:S(2)}, u32[]{:S(2)}) collective-permute-start(bf16[1024,1024]{1,0:T(8,128)(2,1)} %get-tuple-element.79), channel_id=1, source_target_pairs={{0,1},{1,0},{2,3},{3,2},{4,5},{5,4},{6,7},{7,6},{8,9},{9,8},{10,11... | collective-permute-start | bytes 6291464 | tf_op jit(solution)/shard_map/ppermute | solution.py:962
  90.0 90.2 %collective-permute-start.8 = (bf16[1024,1024]{1,0:T(8,128)(2,1)}, bf16[1024,1024]{1,0:T(8,128)(2,1)}, u32[]{:S(2)}, u32[]{:S(2)}) collective-permute-start(bf16[1024,1024]{1,0:T(8,128)(2,1)} %get-tuple-element.81), channel_id=1, source_target_pairs={{0,1},{1,0},{2,3},{3,2},{4,5},{5,4},{6,7},{7,6},{8,9},{9,8},{10,11... | collective-permute-start | bytes 6291464 | tf_op jit(solution)/shard_map/ppermute | solution.py:962
  92.5 113.9 %collective-permute-start.2 = (bf16[512,512]{1,0:T(8,128)(2,1)}, bf16[512,512]{1,0:T(8,128)(2,1)}, u32[]{:S(2)}, u32[]{:S(2)}) collective-permute-start(bf16[512,512]{1,0:T(8,128)(2,1)} %maximum_select_fusion.1), channel_id=1, source_target_pairs={{0,1},{1,0},{2,3},{3,2},{4,5},{5,4},{6,7},{7,6},{8,9},{9,8},{10,11... | collective-permute-start | bytes 1572872 | tf_op jit(solution)/shard_map/ppermute | solution.py:962
  93.0 102.2 %collective-permute-start.3 = (f32[2048]{0:T(1024)S(1)}, f32[2048]{0:T(1024)S(1)}, u32[]{:S(2)}, u32[]{:S(2)}) collective-permute-start(f32[2048]{0:T(1024)S(1)} %copy-done.23), channel_id=1, source_target_pairs={{0,1},{1,0},{2,3},{3,2},{4,5},{5,4},{6,7},{7,6},{8,9},{9,8},{10,11... | collective-permute-start | bytes 24584 | tf_op jit(solution)/shard_map/ppermute | solution.py:962
  115.8 70.8 %copy-start.27 = (s32[8]{0:T(128)S(1)}, s32[8]{0:T(128)}, u32[]{:S(2)}) copy-start(s32[8]{0:T(128)} %copy-done.26) | copy-start | bytes 100
  142.4 64.0 %copy-start.5 = (bf16[2,1024,512]{2,1,0:T(8,128)(2,1)S(1)}, bf16[2,1024,512]{2,1,0:T(8,128)(2,1)}, u32[]{:S(2)}) copy-start(bf16[2,1024,512]{2,1,0:T(8,128)(2,1)} %get-tuple-element.76.out_ref) | copy-start | bytes 6291460
  142.4 66.7 %collective-permute-start.7 = (bf16[1024,1024]{1,0:T(8,128)(2,1)}, bf16[1024,1024]{1,0:T(8,128)(2,1)}, u32[]{:S(2)}, u32[]{:S(2)}) collective-permute-start(bf16[1024,1024]{1,0:T(8,128)(2,1)} %collective-permute-done.6.up_near.refs_14_), channel_id=1, source_target_pairs={{0,2},{2,0},{4,6},{6,4},{8,10},{10,8},{12,14},{14,12},{16,18},{18,... | collective-permute-start | bytes 6291464 | tf_op jit(solution)/shard_map/ppermute | solution.py:970
  180.2 28.9 %collective-permute-start.9 = (bf16[1024,1024]{1,0:T(8,128)(2,1)}, bf16[1024,1024]{1,0:T(8,128)(2,1)}, u32[]{:S(2)}, u32[]{:S(2)}) collective-permute-start(bf16[1024,1024]{1,0:T(8,128)(2,1)} %collective-permute-done.8.down_near.refs_17_), channel_id=1, source_target_pairs={{0,2},{2,0},{4,6},{6,4},{8,10},{10,8},{12,14},{14,12},{16,18},{18,... | collective-permute-start | bytes 6291464 | tf_op jit(solution)/shard_map/ppermute | solution.py:970
  188.4 15.0 %collective-permute-start.4 = (bf16[256,1024]{1,0:T(8,128)(2,1)S(1)}, bf16[256,1024]{1,0:T(8,128)(2,1)}, u32[]{:S(2)}, u32[]{:S(2)}) collective-permute-start(bf16[256,1024]{1,0:T(8,128)(2,1)S(1)} %constant_dynamic-slice_fusion.5), channel_id=1, source_target_pairs={{0,1},{1,0},{2,3},{3,2},{4,5},{5,4},{6,7},{7,6},{8,9},{9,8},{10,11... | collective-permute-start | bytes 1572872 | tf_op jit(solution)/shard_map/ppermute | solution.py:962
  203.3 5.8 collective-permute-start.5
  334.5 24.4 %collective-permute-start.12 = (bf16[512,512]{1,0:T(8,128)(2,1)}, bf16[512,512]{1,0:T(8,128)(2,1)}, u32[]{:S(2)}, u32[]{:S(2)}) collective-permute-start(bf16[512,512]{1,0:T(8,128)(2,1)} %maximum_select_fusion.2), channel_id=1, source_target_pairs={{0,1},{1,0},{2,3},{3,2},{4,5},{5,4},{6,7},{7,6},{8,9},{9,8},{10,11... | collective-permute-start | bytes 1572872 | tf_op jit(solution)/shard_map/ppermute | solution.py:962
  336.4 221.4 %collective-permute-start.10 = (bf16[1024,1024]{1,0:T(8,128)(2,1)}, bf16[1024,1024]{1,0:T(8,128)(2,1)}, u32[]{:S(2)}, u32[]{:S(2)}) collective-permute-start(bf16[1024,1024]{1,0:T(8,128)(2,1)} %get-tuple-element.85), channel_id=1, source_target_pairs={{0,1},{1,0},{2,3},{3,2},{4,5},{5,4},{6,7},{7,6},{8,9},{9,8},{10,11... | collective-permute-start | bytes 6291464 | tf_op jit(solution)/shard_map/ppermute | solution.py:962
  337.8 282.7 %collective-permute-start.11 = (bf16[1536,1024]{1,0:T(8,128)(2,1)}, bf16[1536,1024]{1,0:T(8,128)(2,1)S(1)}, u32[]{:S(2)}, u32[]{:S(2)}) collective-permute-start(bf16[1536,1024]{1,0:T(8,128)(2,1)} %get-tuple-element.86), channel_id=1, source_target_pairs={{0,1},{1,0},{2,3},{3,2},{4,5},{5,4},{6,7},{7,6},{8,9},{9,8},{10,11... | collective-permute-start | bytes 9437192 | tf_op jit(solution)/shard_map/ppermute | solution.py:962
  386.6 99.2 %collective-permute-start.13 = (bf16[3,512,512]{2,1,0:T(8,128)(2,1)}, bf16[3,512,512]{2,1,0:T(8,128)(2,1)}, u32[]{:S(2)}, u32[]{:S(2)}) collective-permute-start(bf16[3,512,512]{2,1,0:T(8,128)(2,1)} %maximum_select_fusion), channel_id=1, source_target_pairs={{0,1},{1,0},{2,3},{3,2},{4,5},{5,4},{6,7},{7,6},{8,9},{9,8},{10,11... | collective-permute-start | bytes 4718600 | tf_op jit(solution)/shard_map/ppermute | solution.py:962
  430.3 135.0 %collective-permute-start.14 = (bf16[1024,1024]{1,0:T(8,128)(2,1)}, bf16[1024,1024]{1,0:T(8,128)(2,1)}, u32[]{:S(2)}, u32[]{:S(2)}) collective-permute-start(bf16[1024,1024]{1,0:T(8,128)(2,1)} %get-tuple-element.114), channel_id=1, source_target_pairs={{0,1},{1,0},{2,3},{3,2},{4,5},{5,4},{6,7},{7,6},{8,9},{9,8},{10,11... | collective-permute-start | bytes 6291464 | tf_op jit(solution)/shard_map/ppermute | solution.py:962
  518.8 25.3 %collective-permute-start.17 = (f32[24,1024]{1,0:T(8,128)S(1)}, f32[24,1024]{1,0:T(8,128)S(1)}, u32[]{:S(2)}, u32[]{:S(2)}) collective-permute-start(f32[24,1024]{1,0:T(8,128)S(1)} %maximum_maximum_fusion), channel_id=1, source_target_pairs={{0,2},{2,0},{4,6},{6,4},{8,10},{10,8},{12,14},{14,12},{16,18},{18,... | collective-permute-start | bytes 294920 | tf_op jit(solution)/shard_map/ppermute | solution.py:995
  543.1 79.9 %collective-permute-start.16 = (bf16[1024,1024]{1,0:T(8,128)(2,1)}, bf16[1024,1024]{1,0:T(8,128)(2,1)}, u32[]{:S(2)}, u32[]{:S(2)}) collective-permute-start(bf16[1024,1024]{1,0:T(8,128)(2,1)} %get-tuple-element.116), channel_id=1, source_target_pairs={{0,1},{1,0},{2,3},{3,2},{4,5},{5,4},{6,7},{7,6},{8,9},{9,8},{10,11... | collective-permute-start | bytes 6291464 | tf_op jit(solution)/shard_map/ppermute | solution.py:962
  544.1 5.1 collective-permute-start.18
  549.3 4.7 collective-permute-start.19
  554.0 64.2 %collective-permute-start.15 = (bf16[512,1024]{1,0:T(8,128)(2,1)}, bf16[512,1024]{1,0:T(8,128)(2,1)}, u32[]{:S(2)}, u32[]{:S(2)}) collective-permute-start(bf16[512,1024]{1,0:T(8,128)(2,1)} %get-tuple-element.115), channel_id=1, source_target_pairs={{0,1},{1,0},{2,3},{3,2},{4,5},{5,4},{6,7},{7,6},{8,9},{9,8},{10,11... | collective-permute-start | bytes 3145736 | tf_op jit(solution)/shard_map/ppermute | solution.py:962
  557.8 6.1 collective-permute-start.20
  560.9 55.8 %copy-start.7 = (f32[2,1024,4]{1,2,0:T(4,128)S(1)}, f32[2,1024,4]{1,2,0:T(4,128)}, u32[]{:S(2)}) copy-start(f32[2,1024,4]{1,2,0:T(4,128)} %param.34) | copy-start | bytes 98308
  560.9 55.8 %copy-start.12 = (f32[2,1024,4]{1,2,0:T(4,128)S(1)}, f32[2,1024,4]{1,2,0:T(4,128)}, u32[]{:S(2)}) copy-start(f32[2,1024,4]{1,2,0:T(4,128)} %param.36) | copy-start | bytes 98308
  560.9 55.8 %copy-start.13 = (f32[2,1024,4]{1,2,0:T(4,128)S(1)}, f32[2,1024,4]{1,2,0:T(4,128)}, u32[]{:S(2)}) copy-start(f32[2,1024,4]{1,2,0:T(4,128)} %param.38) | copy-start | bytes 98308
  560.9 56.5 %copy-start.9 = (f32[2,4,1024]{2,1,0:T(4,128)S(1)}, f32[2,4,1024]{2,1,0:T(4,128)}, u32[]{:S(2)}) copy-start(f32[2,4,1024]{2,1,0:T(4,128)} %param.35) | copy-start | bytes 98308
  560.9 56.5 %copy-start.14 = (f32[2,4,1024]{2,1,0:T(4,128)S(1)}, f32[2,4,1024]{2,1,0:T(4,128)}, u32[]{:S(2)}) copy-start(f32[2,4,1024]{2,1,0:T(4,128)} %param.37) | copy-start | bytes 98308
  561.0 56.5 %copy-start.15 = (f32[2,4,1024]{2,1,0:T(4,128)S(1)}, f32[2,4,1024]{2,1,0:T(4,128)}, u32[]{:S(2)}) copy-start(f32[2,4,1024]{2,1,0:T(4,128)} %param.39) | copy-start | bytes 98308
  563.9 51.7 %collective-permute-start.21 = (f32[24,1024]{1,0:T(8,128)S(1)}, f32[24,1024]{1,0:T(8,128)S(1)}, u32[]{:S(2)}, u32[]{:S(2)}) collective-permute-start(f32[24,1024]{1,0:T(8,128)S(1)} %add.292), channel_id=1, source_target_pairs={{0,1},{1,0},{2,3},{3,2},{4,5},{5,4},{6,7},{7,6},{8,9},{9,8},{10,11... | collective-permute-start | bytes 294920 | tf_op jit(solution)/shard_map/ppermute | solution.py:962
  (19 other events, 200.5 us)
